TPU v7x, 128 devices: a whole 4x4x4 slice. The times are simulated.
128 devices in a mesh: cam: 16 (over y, x), pts: 8 (over z, core).
Axes of the slice: x: 4, y: 4, z: 4, core: 2. Of those that a mesh axis runs over, the one named last changes fastest.
Arguments:
- rhs: float32 [9, 131072], P(None, 'cam'), may hold values from -6 to 6
- cam_block: float32 [9, 9, 131072], P(None, None, 'cam'), as said below
- coupling: bfloat16 [512, 144, 12288], P('pts', None, 'cam'), may hold values from -0.03125 to 0.03125
- point_inverse: float32 [3, 3, 32768], P(None, None, 'pts'), as said below
- precond: float32 [9, 9, 131072], P(None, None, 'cam'), as said below
- tile_index: int32 [512, 64], P('pts', 'cam'), may hold values from 0 to 511
- tile_count: int32 [512, 16], P('pts', 'cam'), may hold values from 1 to 4, as said below
Outputs:
- solution: float32 [9, 131072], P(None, 'cam')
- residual: float32 [9, 131072], P(None, 'cam')
Inputs may be any that keep to these rules, and one draw needn't show every extreme that they name: `tile_count`: every entry is at least 1 and at most 4; both ends occur. `cam_block`: symmetric with a dominant positive diagonal for each camera. `precond`: symmetric with a dominant positive diagonal for each camera. `point_inverse`: symmetric with a dominant positive diagonal for each point.
All inputs are finite; a program needn't handle non-finite values.
Results may differ from a plain program's by a relative error of at most 0.0024.
Values may be sent and summed in bfloat16 or wider, within the bound.
A program may use at most 128 MiB of HBM per device.

v0:
```python
import jax
import jax.numpy as jnp
from jax import lax
from jax.sharding import PartitionSpec as P

ITERS = 3


def camera_tiles(vector):
    comps, count = vector.shape
    return (
        vector.reshape(comps, count // 16, 16).transpose(1, 0, 2).reshape(count // 16, comps * 16)
    )


def camera_cols(tiles):
    count = tiles.shape[0]
    return tiles.reshape(count, 9, 16).transpose(1, 0, 2).reshape(9, count * 16)


def point_cols(tiles):
    count = tiles.shape[0]
    return tiles.reshape(count, 3, 64).transpose(1, 0, 2).reshape(3, count * 64)


def point_tiles(vector):
    count = vector.shape[1] // 64
    return vector.reshape(3, count, 64).transpose(1, 0, 2).reshape(count, 192)


def per_device(rhs, cam_block, coupling, point_inverse, precond, tile_index, tile_count):
    tiles_here, slot_count = tile_index.shape
    cam_count = rhs.shape[1] // 16
    blocks = coupling.reshape(tiles_here, 144, slot_count, 192)
    usable = (jnp.arange(slot_count)[None, :] < tile_count).astype(jnp.bfloat16)
    flat_index = tile_index.reshape(-1)
    onehot_t = (jnp.arange(cam_count)[:, None] == flat_index[None, :]).astype(
        jnp.float32
    ) * usable.reshape(1, -1).astype(jnp.float32)

    def global_sum(value):
        return lax.psum(value, "cam")

    solution = jnp.zeros_like(rhs)
    residual = rhs
    precond_res = jnp.sum(precond * residual[None, :, :], axis=1)
    direction = precond_res
    inner_now = global_sum(jnp.sum(residual * precond_res))
    for iteration in range(ITERS):
        dir_rows = jnp.take(
            camera_tiles(direction.astype(jnp.bfloat16)), flat_index, axis=0
        ).reshape(tiles_here, slot_count, 144)
        dir_rows = dir_rows * usable[:, :, None]
        point_part = jnp.einsum(
            "tckp,tkc->tp", blocks, dir_rows, preferred_element_type=jnp.float32
        )
        point_part = point_cols(point_part)
        summed = lax.psum(point_part.astype(jnp.bfloat16), "cam").astype(jnp.float32)
        solved = jnp.sum(point_inverse * summed[None, :, :], axis=1).astype(jnp.bfloat16)
        contrib = jnp.einsum(
            "tckp,tp->tkc", blocks, point_tiles(solved), preferred_element_type=jnp.float32
        )
        cam_part = jnp.dot(
            onehot_t,
            contrib.reshape(-1, 144),
            precision=lax.Precision.HIGHEST,
            preferred_element_type=jnp.float32,
        )
        image = jnp.sum(cam_block * direction[None, :, :], axis=1) - lax.psum(
            camera_cols(cam_part).astype(jnp.bfloat16), "pts"
        ).astype(jnp.float32)
        step_size = inner_now / global_sum(jnp.sum(direction * image))
        solution = solution + step_size * direction
        residual = residual - step_size * image
        if iteration + 1 < ITERS:
            precond_res = jnp.sum(precond * residual[None, :, :], axis=1)
            inner_new = global_sum(jnp.sum(residual * precond_res))
            direction = precond_res + inner_new / inner_now * direction
            inner_now = inner_new
    return (solution, residual)


def solution(mesh):
    in_specs = (
        P(None, "cam"),
        P(None, None, "cam"),
        P("pts", None, "cam"),
        P(None, None, "pts"),
        P(None, None, "cam"),
        P("pts", "cam"),
        P("pts", "cam"),
    )
    out_specs = (P(None, "cam"), P(None, "cam"))
    return jax.shard_map(
        per_device, mesh=mesh, in_specs=in_specs, out_specs=out_specs, check_vma=False
    )
```

profile of v0, /device:TPU:1, one launch (start us, length us, event | category | flops | bytes accessed | tf_op | source)
XLA Modules:
  0.0 764.9 jit_solution(13054918832175976593)
XLA Ops:
  8.1 3.4 multiply_reduce_fusion.5
  14.6 35.9 %reshape.168 = bf16[64,144,4,192]{3,2,1,0:T(4,128)(2,1)} reshape(bf16[64,144,768]{2,1,0:T(8,128)(2,1)} %param.11) | data formatting | bytes 28311552 | tf_op jit(solution)/shard_map/reshape | solution.py:34
  50.6 9.1 %fusion.7 = bf16[64,1,192,1]{2,1,3,0:T(2,128)(2,1)S(1)} fusion(bf16[64,144,4,192]{3,2,1,0:T(4,128)(2,1)} %reshape.168, bf16[64,4,144,1]{2,1,0,3:T(4,128)(2,1)S(1)} %multiply_bitcast_fusion.2), kind=kOutput, calls=%fused_computation.13 | convolution fusion | flops 14155776 | bytes 14254080 | tf_op jit(solution)/shard_map/tckp,tkc->tp/dot_general | solution.py:54
  60.1 61.9 %psum.85 = bf16[3,4096]{1,0:T(4,128)(2,1)S(1)} all-reduce(bf16[3,4096]{1,0:T(4,128)(2,1)S(1)} %convert_element_type.154), channel_id=1, replica_groups=mesh['cam'=16,'pts'=8] {'cam'}, use_global_device_ids=true, to_apply=%region_4.6 | all-reduce | flops 12288 | bytes 49152 | tf_op jit(solution)/shard_map/psum | solution.py:58
  122.5 16.4 %fusion = f32[64,144,4]{2,1,0:T(8,128)} fusion(f32[64,192]{1,0:T(8,128)S(1)} %copy.66, bf16[64,144,4,192]{3,2,1,0:T(4,128)(2,1)} %reshape.168), kind=kLoop, calls=%fused_computation.6 | loop fusion | flops 21196800 | bytes 14352384
  138.9 4.1 copy.51
  144.6 2.5 convert_element_type.160
  147.2 3.3 multiply_reduce_fusion.4
  150.5 66.3 %all-reduce.5.cloned.1.call-done = bf16[9,8192]{1,0:T(8,128)(2,1)} async-done(((bf16[9,8192]{1,0:T(8,128)(2,1)}), bf16[9,8192]{1,0:T(8,128)(2,1)}) %all-reduce.5.cloned.1.call-update) | async-done | bytes 147472 | tf_op jit(solution)/shard_map/psum | solution.py:69
  218.5 33.9 %all-reduce = (f32[]{:T(128)}, f32[]{:T(128)}) all-reduce(f32[]{:T(128)} %get-tuple-element.4, f32[]{:T(128)} %get-tuple-element.3), channel_id=1, replica_groups=mesh['cam'=16,'pts'=8] {'cam'}, use_global_device_ids=true, to_apply=%region_2.0 | all-reduce | flops 2 | bytes 16 | tf_op jit(solution)/shard_map/psum | solution.py:42
  254.7 3.3 multiply_reduce_fusion.3
  258.8 29.3 %psum.88 = f32[]{:T(128)} all-reduce(f32[]{:T(128)} %multiply_reduce_fusion.9), channel_id=1, replica_groups=mesh['cam'=16,'pts'=8] {'cam'}, use_global_device_ids=true, to_apply=%region_11.13 | all-reduce | flops 1 | bytes 8 | tf_op jit(solution)/shard_map/psum | solution.py:42
  292.5 9.1 %fusion.5 = bf16[64,1,192,1]{2,1,3,0:T(2,128)(2,1)S(1)} fusion(bf16[64,144,4,192]{3,2,1,0:T(4,128)(2,1)} %reshape.168, bf16[64,4,144,1]{2,1,0,3:T(4,128)(2,1)S(1)} %multiply_bitcast_fusion.1), kind=kOutput, calls=%fused_computation.11 | convolution fusion | flops 14155776 | bytes 14254080 | tf_op jit(solution)/shard_map/tckp,tkc->tp/dot_general | solution.py:54
  301.9 57.2 %psum.89 = bf16[3,4096]{1,0:T(4,128)(2,1)S(1)} all-reduce(bf16[3,4096]{1,0:T(4,128)(2,1)S(1)} %convert_element_type.167), channel_id=1, replica_groups=mesh['cam'=16,'pts'=8] {'cam'}, use_global_device_ids=true, to_apply=%region_13.15 | all-reduce | flops 12288 | bytes 49152 | tf_op jit(solution)/shard_map/psum | solution.py:58
  359.6 16.4 %fusion.1 = f32[64,144,4]{2,1,0:T(8,128)} fusion(f32[64,192]{1,0:T(8,128)S(1)} %copy.67, bf16[64,144,4,192]{3,2,1,0:T(4,128)(2,1)} %reshape.168), kind=kLoop, calls=%fused_computation.7 | loop fusion | flops 21196800 | bytes 14352384
  376.0 4.1 copy.58
  381.6 2.5 convert_element_type.173
  384.2 3.3 multiply_reduce_fusion.2
  387.5 78.8 %all-reduce.7.cloned.1.call-done = bf16[9,8192]{1,0:T(8,128)(2,1)} async-done(((bf16[9,8192]{1,0:T(8,128)(2,1)}), bf16[9,8192]{1,0:T(8,128)(2,1)}) %all-reduce.7.cloned.1.call-update) | async-done | bytes 147472 | tf_op jit(solution)/shard_map/psum | solution.py:69
  467.9 34.1 %psum.91 = f32[]{:T(128)} all-reduce(f32[]{:T(128)} %multiply_reduce_fusion.8), channel_id=1, replica_groups=mesh['cam'=16,'pts'=8] {'cam'}, use_global_device_ids=true, to_apply=%region_17.19 | all-reduce | flops 1 | bytes 8 | tf_op jit(solution)/shard_map/psum | solution.py:42
  504.3 3.3 multiply_reduce_fusion.1
  508.4 29.2 %psum.92 = f32[]{:T(128)} all-reduce(f32[]{:T(128)} %multiply_reduce_fusion.7), channel_id=1, replica_groups=mesh['cam'=16,'pts'=8] {'cam'}, use_global_device_ids=true, to_apply=%region_20.22 | all-reduce | flops 1 | bytes 8 | tf_op jit(solution)/shard_map/psum | solution.py:42
  539.5 1.9 add.63
  545.0 9.1 %fusion.3 = bf16[64,1,192,1]{2,1,3,0:T(2,128)(2,1)S(1)} fusion(bf16[64,144,4,192]{3,2,1,0:T(4,128)(2,1)} %reshape.168, bf16[64,4,144,1]{2,1,0,3:T(4,128)(2,1)S(1)} %multiply_bitcast_fusion), kind=kOutput, calls=%fused_computation.9 | convolution fusion | flops 14155776 | bytes 14254080 | tf_op jit(solution)/shard_map/tckp,tkc->tp/dot_general | solution.py:54
  554.5 57.6 %psum.93 = bf16[3,4096]{1,0:T(4,128)(2,1)S(1)} all-reduce(bf16[3,4096]{1,0:T(4,128)(2,1)S(1)} %convert_element_type.178), channel_id=1, replica_groups=mesh['cam'=16,'pts'=8] {'cam'}, use_global_device_ids=true, to_apply=%region_22.24 | all-reduce | flops 12288 | bytes 49152 | tf_op jit(solution)/shard_map/psum | solution.py:58
  612.5 16.4 %fusion.2 = f32[64,144,4]{2,1,0:T(8,128)} fusion(f32[64,192]{1,0:T(8,128)S(1)} %copy.68, bf16[64,144,4,192]{3,2,1,0:T(4,128)(2,1)} %reshape.168), kind=kLoop, calls=%fused_computation.8 | loop fusion | flops 21196800 | bytes 14352384
  628.9 4.1 copy.65
  634.5 2.5 convert_element_type.184
  637.0 3.3 multiply_reduce_fusion
  640.3 78.8 %all-reduce.9.cloned.1.call-done = bf16[9,8192]{1,0:T(8,128)(2,1)} async-done(((bf16[9,8192]{1,0:T(8,128)(2,1)}), bf16[9,8192]{1,0:T(8,128)(2,1)}) %all-reduce.9.cloned.1.call-update) | async-done | bytes 147472 | tf_op jit(solution)/shard_map/psum | solution.py:69
  720.8 33.9 %psum.95 = f32[]{:T(128)} all-reduce(f32[]{:T(128)} %multiply_reduce_fusion.6), channel_id=1, replica_groups=mesh['cam'=16,'pts'=8] {'cam'}, use_global_device_ids=true, to_apply=%region_26.28 | all-reduce | flops 1 | bytes 8 | tf_op jit(solution)/shard_map/psum | solution.py:42
  756.1 2.1 multiply_subtract_fusion
  (88 shorter events, 27.0 us)
Async XLA Ops:
  7.2 209.6 %all-reduce.5.cloned.1.call-start = ((), (), s32[]{:S(2)}) async-start(), calls=%async_computation | async-start | bytes 524288 | tf_op jit(solution)/shard_map/psum | solution.py:69
  8.1 6.4 copy-start.2
  50.6 71.4 %copy-start.1 = (f32[3,3,4096]{2,1,0:T(4,128)S(1)}, f32[3,3,4096]{2,1,0:T(4,128)}, u32[]{:S(2)}) copy-start(f32[3,3,4096]{2,1,0:T(4,128)} %param.12) | copy-start | bytes 442372
  143.2 73.6 %copy-start = (f32[9,8192]{1,0:T(8,128)S(1)}, f32[9,8192]{1,0:T(8,128)}, u32[]{:S(2)}) copy-start(f32[9,8192]{1,0:T(8,128)} %param.9) | copy-start | bytes 884740
  147.1 319.1 %all-reduce.7.cloned.1.call-start = ((), (), s32[]{:S(2)}) async-start(), calls=%async_computation.1 | async-start | bytes 524288 | tf_op jit(solution)/shard_map/psum | solution.py:69
  384.1 335.0 %all-reduce.9.cloned.1.call-start = ((), (), s32[]{:S(2)}) async-start(), calls=%async_computation.2 | async-start | bytes 524288 | tf_op jit(solution)/shard_map/psum | solution.py:69
Sparse Core Ops, SparseCore 0:
  147.3 69.4 all-reduce.4
  384.2 81.9 all-reduce.6
  637.1 81.9 all-reduce.8
where the time goes:
time: 781 us; the launch traced here: 765 us
  blocking collectives  337 us (43%)
  waiting for transfers between devices  224 us (29%)
  other arithmetic  82 us (10%)
  local copies, waits for them, and re-layouts  71.4 us (9%)
  matrix products  29.6 us (4%)
  between operations  20.9 us (3%)
    psum x3, waiting for transfers between devices, per_device(): lax.psum(camera_cols(cam_part).astype(jnp.bfloat16), 'pts')  224 us
    psum x3, blocking collectives, per_device(): lax.psum(point_part.astype(jnp.bfloat16), 'cam').astype(jnp.float32)  177 us
    psum x5, blocking collectives, global_sum(): return lax.psum(value, 'cam')  160 us
    unnamed x6, other arithmetic  49.2 us
    reshape x1, local copies, waits for them, and re-layouts, per_device(): blocks = coupling.reshape(tiles_here, 144, slot_count, 192)  35.9 us
    dot_general x3, matrix products, per_device(): jnp.einsum('tckp,tkc->tp', blocks, dir_rows, preferred_element_type=jnp.f...  27.4 us
  transfers between devices with their start and end apart: 3, of which 3 were waited for; matrix products, arithmetic and copies ran while one was open for 1% of the time, Pallas kernels for 0%

commit v1 on v0

v1 whole, which is shorter than its diff:
```python
import functools

import jax
import jax.numpy as jnp
from jax import lax
from jax.experimental import pallas as pl
from jax.experimental.pallas import tpu as pltpu
from jax.sharding import PartitionSpec as P

ITERS = 3
F32 = jnp.float32
BF16 = jnp.bfloat16
CHUNKS = 16
MESH = pl.DeviceIdType.MESH


def iota(shape, axis):
    return lax.broadcasted_iota(jnp.int32, shape, axis)


def kernel(
    n_cam, n_pts,
    rhs_ref, inv_ref, idx_col_ref, idx_row_ref, cam_hbm, pre_hbm, blk_hbm,
    sol_out, res_out,
    blk, cam_nat, pre_nat, cam_d, pre_d,
    r_ref, z_ref, d_ref, s_ref, q_ref, u_ref, cd_ref,
    pick, place, mask, fold, fold_t, group,
    gath, rows, mid, contrib,
    p_send, p_recv, solved, t_send, t_recv, term, dots,
    blk_sem, cam_sem, pre_sem,
    ps_s, ps_r, so_s, so_r, ts_s, ts_r, te_s, te_r, do_s, do_r,
):
    me_c = lax.axis_index("cam")
    me_p = lax.axis_index("pts")
    blocks = d_ref.shape[0] // 9
    steps = blocks // 8
    tiles = blk.shape[0]
    per_chunk = tiles // CHUNKS

    pre_copy = pltpu.make_async_copy(pre_hbm, pre_nat, pre_sem)
    cam_copy = pltpu.make_async_copy(cam_hbm, cam_nat, cam_sem)

    def blk_copy(c):
        part = pl.ds(c * per_chunk, per_chunk)
        return pltpu.make_async_copy(blk_hbm.at[part], blk.at[part], blk_sem.at[c])

    pre_copy.start()

    def start_chunk(c, carry):
        blk_copy(c).start()
        return carry

    lax.fori_loop(0, CHUNKS, start_chunk, 0)
    cam_copy.start()

    barrier = pltpu.get_barrier_semaphore()

    def cam_peer(k):
        return lax.rem(me_c + k, n_cam)

    def pts_peer(k):
        return lax.rem(me_p + k, n_pts)

    def greet_cam(k, carry):
        pl.semaphore_signal(barrier, inc=1, device_id=(cam_peer(k), me_p), device_id_type=MESH)
        return carry

    def greet_pts(k, carry):
        pl.semaphore_signal(barrier, inc=1, device_id=(me_c, pts_peer(k)), device_id_type=MESH)
        return carry

    lax.fori_loop(1, n_cam, greet_cam, 0)
    lax.fori_loop(1, n_pts, greet_pts, 0)

    def cam_send(k, src, dst, ssem, rsem):
        peer = cam_peer(k)
        return pltpu.make_async_remote_copy(
            src_ref=src(peer), dst_ref=dst.at[me_c], send_sem=ssem.at[peer],
            recv_sem=rsem.at[me_c], device_id=(peer, me_p), device_id_type=MESH,
        )

    def cam_arrive(k, src, dst, ssem, rsem):
        peer = cam_peer(k)
        return pltpu.make_async_remote_copy(
            src_ref=src(peer), dst_ref=dst.at[peer], send_sem=ssem.at[peer],
            recv_sem=rsem.at[peer], device_id=(peer, me_p), device_id_type=MESH,
        )

    def pts_send(k, src, dst, ssem, rsem):
        peer = pts_peer(k)
        return pltpu.make_async_remote_copy(
            src_ref=src(peer), dst_ref=dst.at[me_p], send_sem=ssem.at[peer],
            recv_sem=rsem.at[me_p], device_id=(me_c, peer), device_id_type=MESH,
        )

    def pts_arrive(k, src, dst, ssem, rsem):
        peer = pts_peer(k)
        return pltpu.make_async_remote_copy(
            src_ref=src(peer), dst_ref=dst.at[peer], send_sem=ssem.at[peer],
            recv_sem=rsem.at[peer], device_id=(me_c, peer), device_id_type=MESH,
        )

    def start_all(n, send, *args):
        def body(k, carry):
            send(k, *args).start()
            return carry

        lax.fori_loop(1, n, body, 0)

    def wait_all(n, arrive, *args):
        def body(k, carry):
            copy = arrive(k, *args)
            copy.wait_recv()
            copy.wait_send()
            return carry

        lax.fori_loop(1, n, body, 0)

    idx_col = idx_col_ref[...]
    idx_row = idx_row_ref[...]
    pairs = idx_col.shape[0]
    pick[...] = jnp.where(iota((pairs, blocks), 1) == idx_col // 8, 1.0, 0.0).astype(BF16)
    place[...] = jnp.where(iota((blocks, pairs), 0) == idx_row // 8, 1.0, 0.0).astype(BF16)
    mask[...] = jnp.where(iota((pairs, 128), 1) // 16 == lax.rem(idx_col + 8, 8), 1.0, 0.0)
    at = iota((9 * 128, 144), 0)
    fold[...] = jnp.where(
        iota((9 * 128, 144), 1) == (at // 128) * 16 + lax.rem(at, 16), 1.0, 0.0
    ).astype(BF16)
    at = iota((144, 9 * 128), 1)
    fold_t[...] = jnp.where(
        iota((144, 9 * 128), 0) == (at // 128) * 16 + lax.rem(at, 16), 1.0, 0.0
    ).astype(BF16)
    group[...] = jnp.where(iota((tiles, pairs), 1) // 4 == iota((tiles, pairs), 0), 1.0, 0.0).astype(
        BF16
    )

    def to_dense(src, dst):
        def body(b, carry):
            dst[pl.ds(b, 9, stride=blocks), :] = src[:, pl.ds(pl.multiple_of(b * 128, 128), 128)]
            return carry

        lax.fori_loop(0, blocks, body, 0, unroll=4)

    def to_dense_blocks(src, dst):
        def body(b, carry):
            for i in range(9):
                dst[i, pl.ds(b, 9, stride=blocks), :] = src[
                    i, :, pl.ds(pl.multiple_of(b * 128, 128), 128)
                ]
            return carry

        lax.fori_loop(0, blocks, body, 0)

    def at_rows(j, step):
        return pl.ds(pl.multiple_of(j * blocks + step * 8, 8), 8)

    def apply_rows(mat, vec, i, step):
        total = mat[i, at_rows(0, step), :] * vec[0]
        for j in range(1, 9):
            total = total + mat[i, at_rows(j, step), :] * vec[j]
        return total

    to_dense(rhs_ref, r_ref)
    pre_copy.wait()
    to_dense_blocks(pre_nat, pre_d)

    def first(step, acc):
        r = [r_ref[at_rows(j, step), :] for j in range(9)]
        for i in range(9):
            z = apply_rows(pre_d, r, i, step)
            z_ref[at_rows(i, step), :] = z
            d_ref[at_rows(i, step), :] = z
            acc = acc + r[i] * z
        return acc

    rz = lax.fori_loop(0, steps, first, jnp.zeros((8, 128), F32))
    pl.semaphore_wait(barrier, n_cam + n_pts - 2)

    row8 = iota((8, 768), 0)
    diag = iota((8, 768), 1) // 192 == lax.rem(row8, 4)
    upper = row8 < 4

    inner = None
    for it in range(ITERS):
        last = it + 1 == ITERS
        for j in range(9):
            part = d_ref[j * blocks : (j + 1) * blocks, :].astype(BF16)
            picked = jnp.dot(pick[...], part, preferred_element_type=F32)
            gath[:, j * 128 : (j + 1) * 128] = (picked * mask[...]).astype(BF16)
        rows[...] = jnp.dot(gath[...], fold[...], preferred_element_type=F32)

        def forward(j):
            left = rows[pl.ds(pl.multiple_of(8 * j, 8), 8), :].astype(BF16)
            one = jnp.dot(left, blk[2 * j], preferred_element_type=F32)
            two = jnp.dot(left, blk[2 * j + 1], preferred_element_type=F32)
            mid[pl.ds(pl.multiple_of(8 * j, 8), 8), :] = jnp.where(
                diag, jnp.where(upper, one, two), 0.0
            )

        def forward_chunk(c, carry):
            if it == 0:
                blk_copy(c).wait()
            for k in range(per_chunk // 2):
                forward(c * (per_chunk // 2) + k)
            return carry

        lax.fori_loop(0, CHUNKS, forward_chunk, 0, unroll=1 if it == 0 else 2)
        full = mid[...]
        high = full.astype(BF16)
        low = (full - high.astype(F32)).astype(BF16)
        summed = jnp.dot(group[...], high, preferred_element_type=F32) + jnp.dot(
            group[...], low, preferred_element_type=F32
        )
        summed = summed[:, :384] + summed[:, 384:]
        summed = summed + pltpu.roll(summed, 192, 1)
        slab = tiles // n_cam
        for o in range(n_cam):
            p_send[o] = summed[o * slab : (o + 1) * slab, :]
        own = (lambda peer: p_send.at[peer], p_recv, ps_s, ps_r)
        start_all(n_cam, cam_send, *own)

        if it == 0:
            cam_copy.wait()
            to_dense_blocks(cam_nat, cam_d)

        def cam_apply(step, carry):
            d = [d_ref[at_rows(j, step), :] for j in range(9)]
            for i in range(9):
                cd_ref[at_rows(i, step), :] = apply_rows(cam_d, d, i, step)
            return carry

        lax.fori_loop(0, steps, cam_apply, 0)

        wait_all(n_cam, cam_arrive, *own)
        total = p_send[me_c]
        for k in range(1, n_cam):
            total = total + p_recv[cam_peer(k)]
        answer = inv_ref[0] * total
        for k in (1, 2):
            answer = answer + inv_ref[k] * pltpu.roll(total, 384 - 64 * k, 1)
        solved[me_c] = answer.astype(BF16).astype(F32)
        own = (lambda peer: solved.at[me_c], solved, so_s, so_r)
        start_all(n_cam, cam_send, *own)
        wait_all(n_cam, cam_arrive, *own)

        def backward(j, carry):
            q4 = lax.rem(j, 2) * 2
            one = jnp.broadcast_to(solved[j // 2, pl.ds(q4, 1), :], (8, 384))
            two = jnp.broadcast_to(solved[j // 2, pl.ds(q4 + 1, 1), :], (8, 384))
            both = jnp.where(upper[:, :384], one, two)
            left = jnp.where(diag, jnp.concatenate([both, both], axis=1), 0.0).astype(BF16)
            contract = (((1,), (1,)), ((), ()))
            one = lax.dot_general(left, blk[2 * j], contract, preferred_element_type=F32)
            two = lax.dot_general(left, blk[2 * j + 1], contract, preferred_element_type=F32)
            contrib[pl.ds(pl.multiple_of(8 * j, 8), 8), :] = jnp.where(
                upper[:, :144], one, two
            )
            return carry

        lax.fori_loop(0, tiles // 2, backward, 0, unroll=4)
        contrib_half = contrib[...].astype(BF16)
        for j in range(9):
            lanes = slice(j * 128, (j + 1) * 128)
            wide = jnp.dot(contrib_half, fold_t[:, lanes], preferred_element_type=F32)
            wide = (wide * mask[...]).astype(BF16)
            put = jnp.dot(place[...], wide, preferred_element_type=F32)
            for o in range(n_pts):
                t_send[o, :, lanes] = put[o * 8 : (o + 1) * 8, :].astype(BF16)
        own = (lambda peer: t_send.at[peer], t_recv, ts_s, ts_r)
        start_all(n_pts, pts_send, *own)
        wait_all(n_pts, pts_arrive, *own)
        total = t_send[me_p].astype(F32)
        for k in range(1, n_pts):
            total = total + t_recv[pts_peer(k)].astype(F32)
        term[me_p] = total.astype(BF16)
        own = (lambda peer: term.at[me_p], term, te_s, te_r)
        start_all(n_pts, pts_send, *own)
        wait_all(n_pts, pts_arrive, *own)

        def image(step, acc):
            dq, zq, uq = acc
            q = []
            for i in range(9):
                value = cd_ref[at_rows(i, step), :] - term[step, :, i * 128 : (i + 1) * 128].astype(
                    F32
                )
                q_ref[at_rows(i, step), :] = value
                q.append(value)
                dq = dq + d_ref[at_rows(i, step), :] * value
            if not last:
                for i in range(9):
                    u = apply_rows(pre_d, q, i, step)
                    u_ref[at_rows(i, step), :] = u
                    zq = zq + z_ref[at_rows(i, step), :] * q[i]
                    uq = uq + u * q[i]
            return dq, zq, uq

        zero = jnp.zeros((8, 128), F32)
        dq, zq, uq = lax.fori_loop(0, steps, image, (zero, zero, zero))
        dots[me_c, 0:1, :] = jnp.sum(dq, axis=0, keepdims=True)
        dots[me_c, 1:2, :] = jnp.sum(zq, axis=0, keepdims=True)
        dots[me_c, 2:3, :] = jnp.sum(uq, axis=0, keepdims=True)
        dots[me_c, 3:4, :] = jnp.sum(rz, axis=0, keepdims=True)
        own = (lambda peer: dots.at[me_c], dots, do_s, do_r)
        start_all(n_cam, cam_send, *own)
        wait_all(n_cam, cam_arrive, *own)
        total = dots[0]
        for k in range(1, n_cam):
            total = total + dots[k]
        total = jnp.sum(total, axis=1, keepdims=True)
        if it == 0:
            inner = total[3:4]
        size = inner / total[0:1]
        alpha = jnp.broadcast_to(size, (8, 128))
        if not last:
            inner_new = inner - 2.0 * size * total[1:2] + size * size * total[2:3]
            beta = jnp.broadcast_to(inner_new / inner, (8, 128))
            inner = inner_new

        def update(step, carry):
            for i in range(9):
                at_i = at_rows(i, step)
                d = d_ref[at_i, :]
                s = alpha * d
                if it > 0:
                    s = s_ref[at_i, :] + s
                s_ref[at_i, :] = s
                r_ref[at_i, :] = r_ref[at_i, :] - alpha * q_ref[at_i, :]
                if not last:
                    z = z_ref[at_i, :] - alpha * u_ref[at_i, :]
                    z_ref[at_i, :] = z
                    d_ref[at_i, :] = z + beta * d
            return carry

        lax.fori_loop(0, steps, update, 0)

    def from_dense(b, carry):
        lanes = pl.ds(pl.multiple_of(b * 128, 128), 128)
        sol_out[:, lanes] = s_ref[pl.ds(b, 9, stride=blocks), :]
        res_out[:, lanes] = r_ref[pl.ds(b, 9, stride=blocks), :]
        return carry

    lax.fori_loop(0, blocks, from_dense, 0, unroll=4)


def per_device(n_cam, n_pts, rhs, cam_block, coupling, point_inverse, precond, tile_index, tile_count):
    tiles, slots = tile_index.shape
    cams = rhs.shape[1]
    blocks = cams // 128
    slab = tiles // n_cam
    used = jnp.arange(slots)[None, :] < tile_count
    index = jnp.where(used, tile_index, -8)
    pairs = tiles * slots
    own = lax.dynamic_slice_in_dim(point_inverse, lax.axis_index("cam") * slab * 64, slab * 64, 2)
    own = own.reshape(3, 3, slab, 64)
    turned = [
        jnp.concatenate([own[i % 3, (i + k) % 3] for i in range(6)], axis=1) for k in range(3)
    ]
    inv = jnp.stack(turned)
    vec = pltpu.VMEM((9 * blocks, 128), F32)
    whole = pl.BlockSpec(memory_space=pltpu.VMEM)
    hbm = pl.BlockSpec(memory_space=pl.ANY)
    dma = pltpu.SemaphoreType.DMA
    return pl.pallas_call(
        functools.partial(kernel, n_cam, n_pts),
        out_shape=(jax.ShapeDtypeStruct(rhs.shape, F32), jax.ShapeDtypeStruct(rhs.shape, F32)),
        in_specs=[whole, whole, whole, whole, hbm, hbm, hbm],
        out_specs=(whole, whole),
        scratch_shapes=[
            pltpu.VMEM(coupling.shape, BF16),
            pltpu.VMEM(cam_block.shape, F32),
            pltpu.VMEM(precond.shape, F32),
            pltpu.VMEM((9, 9 * blocks, 128), F32),
            pltpu.VMEM((9, 9 * blocks, 128), F32),
            vec, vec, vec, vec, vec, vec, vec,
            pltpu.VMEM((pairs, blocks), BF16),
            pltpu.VMEM((blocks, pairs), BF16),
            pltpu.VMEM((pairs, 128), F32),
            pltpu.VMEM((9 * 128, 144), BF16),
            pltpu.VMEM((144, 9 * 128), BF16),
            pltpu.VMEM((tiles, pairs), BF16),
            pltpu.VMEM((pairs, 9 * 128), BF16),
            pltpu.VMEM((pairs, 144), F32),
            pltpu.VMEM((pairs, 768), F32),
            pltpu.VMEM((pairs, 144), F32),
            pltpu.VMEM((n_cam, slab, 384), F32),
            pltpu.VMEM((n_cam, slab, 384), F32),
            pltpu.VMEM((n_cam, slab, 384), F32),
            pltpu.VMEM((n_pts, blocks // n_pts, 9 * 128), BF16),
            pltpu.VMEM((n_pts, blocks // n_pts, 9 * 128), BF16),
            pltpu.VMEM((n_pts, blocks // n_pts, 9 * 128), BF16),
            pltpu.VMEM((n_cam, 4, 128), F32),
            dma((CHUNKS,)), dma, dma,
            dma((n_cam,)), dma((n_cam,)), dma((n_cam,)), dma((n_cam,)),
            dma((n_pts,)), dma((n_pts,)), dma((n_pts,)), dma((n_pts,)),
            dma((n_cam,)), dma((n_cam,)),
        ],
        compiler_params=pltpu.CompilerParams(
            collective_id=0, has_side_effects=True, vmem_limit_bytes=58 * 2**20
        ),
    )(rhs, inv, index.reshape(pairs, 1), index.reshape(1, pairs), cam_block, precond, coupling)


def solution(mesh):
    in_specs = (
        P(None, "cam"),
        P(None, None, "cam"),
        P("pts", None, "cam"),
        P(None, None, "pts"),
        P(None, None, "cam"),
        P("pts", "cam"),
        P("pts", "cam"),
    )
    out_specs = (P(None, "cam"), P(None, "cam"))
    body = functools.partial(per_device, mesh.shape["cam"], mesh.shape["pts"])
    return jax.shard_map(body, mesh=mesh, in_specs=in_specs, out_specs=out_specs, check_vma=False)
```

time: 781 us -> 123 us (0.16); the launches traced: 765 us -> 123 us
  blocking collectives: 337 us -> 0 us
  waiting for transfers between devices: 224 us -> 0 us
  Pallas kernels: 0 us -> 115 us
  other arithmetic: 82 us -> 1.34 us
  local copies, waits for them, and re-layouts: 71.4 us -> 5.87 us
  matrix products: 29.6 us -> 0 us
  between operations: 20.9 us -> 0.66 us
    psum x8 -> x0, blocking collectives: 337 us -> none  [the longest x3 177 us: per_device(): lax.psum(point_part.astype(jnp.bfloat16), 'cam').astype(jnp.float32)]
    psum x3 -> x0, waiting for transfers between devices: 224 us -> none  [per_device(): lax.psum(camera_cols(cam_part).astype(jnp.bfloat16), 'pts')]
    pallas_call x0 -> x1, Pallas kernels: none -> 115 us  [per_device(): pl.pallas_call(functools.partial(kernel, n_cam, n_pts), out_shape=(jax.Sh...]
    unnamed x6 -> x0, other arithmetic: 49.2 us -> none
    reshape x10 -> x3, local copies, waits for them, and re-layouts: 37.7 us -> 1.52 us  [the longest x1 0.75 us: per_device(): index.reshape(pairs, 1)]
    dot_general x6 -> x0, matrix products: 29.6 us -> none  [the longest x3 27.4 us: per_device(): jnp.einsum('tckp,tkc->tp', blocks, dir_rows, preferred_element_type=jnp.f...]
    reduce_sum x14 -> x0, other arithmetic: 26.9 us -> none  [the longest x3 10 us: per_device(): precond_res = jnp.sum(precond * residual[None, :, :], axis=1)]
    dot_general x9 -> x0, local copies, waits for them, and re-layouts: 12.9 us -> none  [the longest x3 12.3 us: per_device(): jnp.einsum('tckp,tp->tkc', blocks, point_tiles(solved), preferred_element...]
  transfers between devices with their start and end apart: 3 -> 0, of which waited for: 3 -> 0; matrix products, arithmetic and copies ran while one was open for 1% -> 0% of each run, Pallas kernels for 0% -> 0%
where the time goes in v1:
time: 123 us
  Pallas kernels  115 us (93%)
  local copies, waits for them, and re-layouts  5.87 us (5%)
  other arithmetic  1.34 us (1%)
    pallas_call x1, Pallas kernels, per_device(): pl.pallas_call(functools.partial(kernel, n_cam, n_pts), out_shape=(jax.Sh...  115 us
    unnamed x4, local copies, waits for them, and re-layouts  3.96 us

profile of v1, /device:TPU:1, one launch (start us, length us, event | category | flops | bytes accessed | tf_op | source)
XLA Modules:
  0.0 122.7 jit_solution(8861495083450045537)
XLA Ops:
  0.6 0.0 copy-start
  0.7 0.7 fusion
  1.4 0.2 copy-done
  1.6 0.1 reshape.13
  1.7 0.1 concatenate.9
  1.8 0.1 concatenate.11
  1.9 0.1 concatenate.10
  2.0 0.6 pad_maximum_fusion.inv_ref
  2.6 0.1 copy.11
  2.7 0.7 reshape.15.idx_row_ref
  3.4 0.7 reshape.16.idx_col_ref
  4.1 114.8 %shard_map.86 = (f32[9,8192]{1,0:T(8,128)}, f32[9,8192]{1,0:T(8,128)}) custom-call(f32[9,8192]{1,0:T(8,128)} %rhs_ref.1, f32[3,4,384]{2,1,0:T(4,128)} %pad_maximum_fusion.inv_ref, s32[256,1]{1,0:T(8,128)} %reshape.16.idx_col_ref, s32[1,256]{1,0:T(1,128)} %reshape.15.idx_row_ref, f32[9,9,8192]{2,1,0:T(8,128)} %cam_hbm.1, f32[9,9,8192]{2,1,0:T(8,128)} %pre_hbm.1, ...), custom_call_target="tpu_custom_call" | custom-call | tf_op jit(solution)/shard_map/pallas_call | solution.py:364
  119.0 1.9 %copy.16 = f32[9,8192]{1,0:T(8,128)} copy(f32[9,8192]{1,0:T(8,128)} %get-tuple-element.13) | data formatting | bytes 589824
  120.8 1.9 %copy.17 = f32[9,8192]{1,0:T(8,128)} copy(f32[9,8192]{1,0:T(8,128)} %get-tuple-element.14) | data formatting | bytes 589824
  (2 shorter events, 0.0 us)
Async XLA Ops:
  0.6 1.0 copy-start

commit v2 on v0

v2 whole, which is shorter than its diff:
```python
import functools

import jax
import jax.numpy as jnp
from jax import lax
from jax.experimental import pallas as pl
from jax.experimental.pallas import tpu as pltpu
from jax.sharding import PartitionSpec as P

ITERS = 3
F32 = jnp.float32
BF16 = jnp.bfloat16
CHUNKS = 16
HALVES = 2
MESH = pl.DeviceIdType.MESH


def iota(shape, axis):
    return lax.broadcasted_iota(jnp.int32, shape, axis)


def one_hot(where):
    return jnp.where(where, 1.0, 0.0).astype(BF16)


def kernel(
    n_cam, n_pts,
    idx_ref, count_ref, rhs_hbm, inv_hbm, cam_hbm, pre_hbm, blk_hbm,
    sol_out, res_out,
    blk, cam_nat, pre_nat, rhs_nat, inv_nat, cam_d, pre_d, inv_d,
    r_ref, z_ref, d_ref, s_ref, q_ref, cz_ref,
    pick, place, mask, fold, fold_t, group,
    gath, rows, mid, contrib, even, odd,
    p_send, p_recv, z_all, t_send, t_recv, dots_c, dots_p, out_nat,
    blk_sem, cam_sem, pre_sem, rhs_sem, inv_sem,
    ps_s, ps_r, z_s, z_r, t_s, t_r, dc_s, dc_r, dp_s, dp_r, so_s, so_r, re_s, re_r,
):
    me_c = lax.axis_index("cam")
    me_p = lax.axis_index("pts")
    tiles = blk.shape[0]
    pairs = tiles // 2
    slots = 4 * tiles
    per_half = pairs // HALVES
    per_chunk = tiles // CHUNKS
    blocks = place.shape[0]
    own = rhs_nat.shape[1]
    lanes_here = pl.ds(pl.multiple_of(me_p * own, own), own)

    pre_copy = pltpu.make_async_copy(pre_hbm.at[:, :, lanes_here], pre_nat, pre_sem)
    cam_copy = pltpu.make_async_copy(cam_hbm.at[:, :, lanes_here], cam_nat, cam_sem)
    rhs_copy = pltpu.make_async_copy(rhs_hbm.at[:, lanes_here], rhs_nat, rhs_sem)
    inv_copy = pltpu.make_async_copy(inv_hbm, inv_nat, inv_sem)

    def blk_copy(c):
        part = pl.ds(c * per_chunk, per_chunk)
        return pltpu.make_async_copy(blk_hbm.at[part], blk.at[part], blk_sem.at[c])

    rhs_copy.start()
    pre_copy.start()

    def start_chunk(c, carry):
        blk_copy(c).start()
        return carry

    lax.fori_loop(0, CHUNKS, start_chunk, 0)
    inv_copy.start()
    cam_copy.start()

    barrier = pltpu.get_barrier_semaphore()

    def cam_peer(k):
        return lax.rem(me_c + k, n_cam)

    def pts_peer(k):
        return lax.rem(me_p + k, n_pts)

    def greet_cam(k, carry):
        pl.semaphore_signal(barrier, inc=1, device_id=(cam_peer(k), me_p), device_id_type=MESH)
        return carry

    def greet_pts(k, carry):
        pl.semaphore_signal(barrier, inc=1, device_id=(me_c, pts_peer(k)), device_id_type=MESH)
        return carry

    lax.fori_loop(1, n_cam, greet_cam, 0)
    lax.fori_loop(1, n_pts, greet_pts, 0)

    def cam_copy_to(peer, slot, src, dst, ssem, rsem):
        return pltpu.make_async_remote_copy(
            src_ref=src(peer), dst_ref=dst(slot), send_sem=ssem.at[peer],
            recv_sem=rsem.at[slot], device_id=(peer, me_p), device_id_type=MESH,
        )

    def pts_copy_to(peer, slot, src, dst, ssem, rsem):
        return pltpu.make_async_remote_copy(
            src_ref=src(peer), dst_ref=dst(slot), send_sem=ssem.at[peer],
            recv_sem=rsem.at[slot], device_id=(me_c, peer), device_id_type=MESH,
        )

    def start_cam(*args):
        def body(k, carry):
            cam_copy_to(cam_peer(k), me_c, *args).start()
            return carry

        lax.fori_loop(1, n_cam, body, 0)

    def wait_cam(*args):
        def body(k, carry):
            copy = cam_copy_to(cam_peer(k), cam_peer(k), *args)
            copy.wait_recv()
            copy.wait_send()
            return carry

        lax.fori_loop(1, n_cam, body, 0)

    def start_pts(*args):
        def body(k, carry):
            pts_copy_to(pts_peer(k), me_p, *args).start()
            return carry

        lax.fori_loop(1, n_pts, body, 0)

    def wait_pts(*args):
        def body(k, carry):
            copy = pts_copy_to(pts_peer(k), pts_peer(k), *args)
            copy.wait_recv()
            copy.wait_send()
            return carry

        lax.fori_loop(1, n_pts, body, 0)

    def part(j):
        return slice(8 * j, 8 * j + 8)

    def to_dense(src, dst):
        for b in range(8):
            dst[pl.ds(b, 9, stride=8), :] = src[:, 128 * b : 128 * b + 128]

    def to_dense_blocks(src, dst):
        def body(i, carry):
            for b in range(8):
                dst[i, pl.ds(b, 9, stride=8), :] = src[i, :, 128 * b : 128 * b + 128]
            return carry

        lax.fori_loop(0, 9, body, 0)

    def apply_block(mat, vec):
        out = []
        for i in range(9):
            total = mat[i, part(0), :] * vec[0]
            for j in range(1, 9):
                total = total + mat[i, part(j), :] * vec[j]
            out.append(total)
        return out

    def precondition(r):
        z = apply_block(pre_d, r)
        gamma = r[0] * z[0]
        for j in range(1, 9):
            gamma = gamma + r[j] * z[j]
        for j in range(9):
            z_ref[part(j), :] = z[j]
            z_all[me_p, :, 128 * j : 128 * j + 128] = z[j].astype(BF16)
        return gamma

    z_args = (lambda peer: z_all.at[me_p], lambda slot: z_all.at[slot], z_s, z_r)

    rhs_copy.wait()
    to_dense(rhs_nat, r_ref)
    pre_copy.wait()
    to_dense_blocks(pre_nat, pre_d)
    gamma = precondition([r_ref[part(j), :] for j in range(9)])
    pl.semaphore_wait(barrier, n_cam + n_pts - 2)
    start_pts(*z_args)

    index = idx_ref[...]
    used = iota((tiles, 4), 1) < count_ref[...]
    spread = one_hot(iota((slots, tiles), 0) // 4 == iota((slots, tiles), 1))
    here = iota((slots, 4), 1) == lax.rem(iota((slots, 4), 0), 4)

    def column(value):
        wide = jnp.dot(spread, value.astype(F32).astype(BF16), preferred_element_type=F32)
        return jnp.sum(jnp.where(here, wide, 0.0), axis=1, keepdims=True)

    chosen = jnp.where(
        iota((slots, blocks), 1).astype(F32) == column(jnp.where(used, index // 8, -1)), 1.0, 0.0
    )
    pick[...] = chosen.astype(BF16)
    place[...] = jnp.transpose(chosen).astype(BF16)
    mask[...] = jnp.where(
        (iota((slots, 128), 1) // 16).astype(F32) == column(lax.rem(index, 8)), 1.0, 0.0
    )
    at = iota((9 * 128, 144), 0)
    fold[...] = one_hot(iota((9 * 128, 144), 1) == (at // 128) * 16 + lax.rem(at, 16))
    at = iota((144, 9 * 128), 1)
    fold_t[...] = one_hot(iota((144, 9 * 128), 0) == (at // 128) * 16 + lax.rem(at, 16))
    row = iota((2 * per_half, 8 * per_half), 0)
    col = iota((2 * per_half, 8 * per_half), 1)
    group[...] = one_hot(
        (col // 8 == lax.rem(row, per_half)) & (lax.rem(col, 8) // 4 == row // per_half)
    )
    inv_copy.wait()

    def inv_dense(b, carry):
        for i in range(3):
            inv_d[i, pl.ds(b, 3, stride=pairs), :] = inv_nat[
                i, :, pl.ds(pl.multiple_of(b * 128, 128), 128)
            ]
        return carry

    lax.fori_loop(0, pairs, inv_dense, 0, unroll=4)
    cam_copy.wait()
    to_dense_blocks(cam_nat, cam_d)

    row8 = iota((8, 768), 0)
    diag = iota((8, 768), 1) // 192 == lax.rem(row8, 4)
    upper = row8 < 4
    first_tile = lax.rem(iota((per_half, 384), 1), 128) < 64
    order = (0, 2, 1)

    gamma_old = None
    alpha_old = None
    for it in range(ITERS):
        last = it + 1 == ITERS
        parity = it % 2
        wait_pts(*z_args)
        for j in range(9):
            wide = z_all[:, :, 128 * j : 128 * j + 128].astype(F32).reshape(blocks, 128)
            picked = jnp.dot(pick[...], wide.astype(BF16), preferred_element_type=F32)
            gath[:, 128 * j : 128 * j + 128] = (picked * mask[...]).astype(BF16)
        rows[...] = jnp.dot(gath[...], fold[...], preferred_element_type=F32)

        def forward(j, h):
            left = rows[pl.ds(pl.multiple_of(8 * j, 8), 8), :].astype(BF16)
            one = jnp.dot(left, blk[2 * j], preferred_element_type=F32)
            two = jnp.dot(left, blk[2 * j + 1], preferred_element_type=F32)
            both = jnp.where(diag, jnp.where(upper, one, two), 0.0)
            mid[pl.ds(pl.multiple_of(8 * (j - h * per_half), 8), 8), :] = (
                both[:, :384] + both[:, 384:]
            )

        def p_args(h):
            return (
                lambda peer: p_send.at[h],
                lambda slot: p_recv.at[parity, h, slot],
                ps_s.at[h],
                ps_r.at[parity, h],
            )

        for h in range(HALVES):
            if it == 0:

                def forward_chunk(c, carry):
                    blk_copy(c).wait()
                    for k in range(per_chunk // 2):
                        forward(c * (per_chunk // 2) + k, h)
                    return carry

                some = CHUNKS // HALVES
                lax.fori_loop(h * some, (h + 1) * some, forward_chunk, 0)
            else:

                def forward_four(c, carry):
                    for k in range(4):
                        forward(4 * c + k, h)
                    return carry

                some = per_half // 4
                lax.fori_loop(h * some, (h + 1) * some, forward_four, 0)
            full = mid[...]
            high = full.astype(BF16)
            low = (full - high.astype(F32)).astype(BF16)
            summed = jnp.dot(group[...], high, preferred_element_type=F32) + jnp.dot(
                group[...], low, preferred_element_type=F32
            )
            summed = summed + pltpu.roll(summed, 192, 1)
            p_send[h] = jnp.where(
                first_tile, summed[:per_half], pltpu.roll(summed[per_half:], 64, 1)
            ).astype(BF16)
            start_cam(*p_args(h))

        z = [z_ref[part(j), :] for j in range(9)]
        cz = apply_block(cam_d, z)
        curve = z[0] * cz[0]
        for j in range(1, 9):
            curve = curve + z[j] * cz[j]
        for j in range(9):
            cz_ref[part(j), :] = cz[j]
        dots_c[parity, me_c, 0:1, :] = jnp.sum(gamma, axis=0, keepdims=True)
        dots_c[parity, me_c, 1:2, :] = jnp.sum(curve, axis=0, keepdims=True)
        dc_args = (
            lambda peer: dots_c.at[parity, me_c],
            lambda slot: dots_c.at[parity, slot],
            dc_s,
            dc_r.at[parity],
        )
        start_cam(*dc_args)

        def backward(j):
            both = jnp.where(
                upper[:, :384],
                jnp.broadcast_to(even[pl.ds(j, 1), :], (8, 384)),
                jnp.broadcast_to(odd[pl.ds(j, 1), :], (8, 384)),
            )
            left = jnp.where(diag, jnp.concatenate([both, both], axis=1), 0.0).astype(BF16)
            contract = (((1,), (1,)), ((), ()))
            one = lax.dot_general(left, blk[2 * j], contract, preferred_element_type=F32)
            two = lax.dot_general(left, blk[2 * j + 1], contract, preferred_element_type=F32)
            contrib[pl.ds(pl.multiple_of(8 * j, 8), 8), :] = jnp.where(upper[:, :144], one, two)

        energy = jnp.zeros((per_half, 128), F32)
        for h in range(HALVES):
            wait_cam(*p_args(h))
            total = p_send[h].astype(F32)
            for k in range(1, n_cam):
                total = total + p_recv[parity, h, cam_peer(k)].astype(F32)
            sums = [None] * 3
            for place_i, i in enumerate(order):
                sums[i] = total[:, 128 * place_i : 128 * place_i + 128]
            here_h = slice(h * per_half, (h + 1) * per_half)
            answers = []
            for i in order:
                answer = jnp.zeros((per_half, 128), F32)
                for j in range(3):
                    at_j = slice(j * pairs + h * per_half, j * pairs + (h + 1) * per_half)
                    answer = answer + inv_d[i, at_j, :] * sums[j]
                answer = answer.astype(BF16).astype(F32)
                energy = energy + answer * sums[i]
                answers.append(answer)
            answer = jnp.concatenate(answers, axis=1)
            a = jnp.where(first_tile, answer, 0.0)
            even[here_h, :] = a + pltpu.roll(a, 192, 1)
            a = pltpu.roll(jnp.where(first_tile, 0.0, answer), 320, 1)
            odd[here_h, :] = a + pltpu.roll(a, 192, 1)
            if h + 1 == HALVES:
                wait_cam(*dc_args)
                total = dots_c[parity, 0]
                for k in range(1, n_cam):
                    total = total + dots_c[parity, k]
                dots_p[me_p, 0:2, :] = total[0:2]
                dots_p[me_p, 2:3, :] = jnp.sum(energy, axis=0, keepdims=True)
                dp_args = (
                    lambda peer: dots_p.at[me_p],
                    lambda slot: dots_p.at[slot],
                    dp_s,
                    dp_r,
                )
                start_pts(*dp_args)

            def backward_four(c, carry):
                for k in range(4):
                    backward(4 * c + k)
                return carry

            some = per_half // 4
            lax.fori_loop(h * some, (h + 1) * some, backward_four, 0)

        contrib_half = contrib[...].astype(BF16)
        for j in range(9):
            lanes = slice(j * 128, (j + 1) * 128)
            wide = jnp.dot(contrib_half, fold_t[:, lanes], preferred_element_type=F32)
            wide = (wide * mask[...]).astype(BF16)
            put = jnp.dot(place[...], wide, preferred_element_type=F32)
            for o in range(n_pts):
                t_send[o, :, lanes] = put[o * 8 : (o + 1) * 8, :].astype(BF16)
        t_args = (lambda peer: t_send.at[peer], lambda slot: t_recv.at[slot], t_s, t_r)
        start_pts(*t_args)

        wait_pts(*dp_args)
        total = dots_p[0, 0:3]
        for k in range(1, n_pts):
            total = total + dots_p[k, 0:3]
        total = jnp.sum(total, axis=1, keepdims=True)
        gamma_now = total[0:1]
        curve_now = total[1:2] - total[2:3]
        if it == 0:
            alpha = gamma_now / curve_now
        else:
            beta = gamma_now / gamma_old
            alpha = gamma_now / (curve_now - beta * gamma_now / alpha_old)
            beta_all = jnp.broadcast_to(beta, (8, 128))
        gamma_old, alpha_old = gamma_now, alpha
        alpha_all = jnp.broadcast_to(alpha, (8, 128))
        for j in range(9):
            if it == 0:
                d = z[j]
                s = alpha_all * d
                q = cz[j]
            else:
                d = z_ref[part(j), :] + beta_all * d_ref[part(j), :]
                s = s_ref[part(j), :] + alpha_all * d
                q = cz_ref[part(j), :] + beta_all * q_ref[part(j), :]
            d_ref[part(j), :] = d
            s_ref[part(j), :] = s
            q_ref[part(j), :] = q

        def to_native(src, which, out):
            for b in range(8):
                out_nat[which, :, 128 * b : 128 * b + 128] = src[pl.ds(b, 9, stride=8), :]
            out[:, lanes_here] = out_nat[which]

        def out_args(which, out, ssem, rsem):
            return (
                lambda peer: out_nat.at[which],
                lambda slot: out.at[:, pl.ds(pl.multiple_of(slot * own, own), own)],
                ssem,
                rsem,
            )

        if last:
            to_native(s_ref, 0, sol_out)
            start_pts(*out_args(0, sol_out, so_s, so_r))

        wait_pts(*t_args)
        r = []
        for j in range(9):
            lanes = slice(j * 128, (j + 1) * 128)
            total = t_send[me_p, :, lanes].astype(F32)
            for k in range(1, n_pts):
                total = total + t_recv[pts_peer(k), :, lanes].astype(F32)
            q = q_ref[part(j), :] - total
            q_ref[part(j), :] = q
            value = r_ref[part(j), :] - alpha_all * q
            r_ref[part(j), :] = value
            r.append(value)
        if not last:
            gamma = precondition(r)
            start_pts(*z_args)
        else:
            to_native(r_ref, 1, res_out)
            start_pts(*out_args(1, res_out, re_s, re_r))
            wait_pts(*out_args(0, sol_out, so_s, so_r))
            wait_pts(*out_args(1, res_out, re_s, re_r))


def per_device(n_cam, n_pts, rhs, cam_block, coupling, point_inverse, precond, tile_index, tile_count):
    tiles, slots = tile_index.shape
    cams = rhs.shape[1]
    blocks = cams // 128
    here = cams // n_pts
    pairs = tiles * slots
    half = tiles // 2 // HALVES
    vec = pltpu.VMEM((72, 128), F32)
    whole = pl.BlockSpec(memory_space=pltpu.VMEM)
    hbm = pl.BlockSpec(memory_space=pl.ANY)
    dma = pltpu.SemaphoreType.DMA
    slab = pltpu.VMEM((n_pts, 8, 9 * 128), BF16)
    return pl.pallas_call(
        functools.partial(kernel, n_cam, n_pts),
        out_shape=(jax.ShapeDtypeStruct(rhs.shape, F32), jax.ShapeDtypeStruct(rhs.shape, F32)),
        in_specs=[whole, whole, hbm, hbm, hbm, hbm, hbm],
        out_specs=(whole, whole),
        scratch_shapes=[
            pltpu.VMEM(coupling.shape, BF16),
            pltpu.VMEM((9, 9, here), F32),
            pltpu.VMEM((9, 9, here), F32),
            pltpu.VMEM((9, here), F32),
            pltpu.VMEM(point_inverse.shape, F32),
            pltpu.VMEM((9, 72, 128), F32),
            pltpu.VMEM((9, 72, 128), F32),
            pltpu.VMEM((3, 3 * tiles // 2, 128), F32),
            vec, vec, vec, vec, vec, vec,
            pltpu.VMEM((pairs, blocks), BF16),
            pltpu.VMEM((blocks, pairs), BF16),
            pltpu.VMEM((pairs, 128), F32),
            pltpu.VMEM((9 * 128, 144), BF16),
            pltpu.VMEM((144, 9 * 128), BF16),
            pltpu.VMEM((2 * half, 8 * half), BF16),
            pltpu.VMEM((pairs, 9 * 128), BF16),
            pltpu.VMEM((pairs, 144), F32),
            pltpu.VMEM((8 * half, 384), F32),
            pltpu.VMEM((pairs, 144), F32),
            pltpu.VMEM((tiles // 2, 384), F32),
            pltpu.VMEM((tiles // 2, 384), F32),
            pltpu.VMEM((HALVES, half, 384), BF16),
            pltpu.VMEM((2, HALVES, n_cam, half, 384), BF16),
            slab, slab, slab,
            pltpu.VMEM((2, n_cam, 2, 128), F32),
            pltpu.VMEM((n_pts, 4, 128), F32),
            pltpu.VMEM((2, 9, here), F32),
            dma((CHUNKS,)), dma, dma, dma, dma,
            dma((HALVES, n_cam)), dma((2, HALVES, n_cam)),
            dma((n_pts,)), dma((n_pts,)),
            dma((n_pts,)), dma((n_pts,)),
            dma((n_cam,)), dma((2, n_cam)),
            dma((n_pts,)), dma((n_pts,)),
            dma((n_pts,)), dma((n_pts,)),
            dma((n_pts,)), dma((n_pts,)),
        ],
        compiler_params=pltpu.CompilerParams(
            collective_id=0, has_side_effects=True, vmem_limit_bytes=48 * 2**20
        ),
    )(tile_index, tile_count, rhs, point_inverse, cam_block, precond, coupling)


def solution(mesh):
    in_specs = (
        P(None, "cam"),
        P(None, None, "cam"),
        P("pts", None, "cam"),
        P(None, None, "pts"),
        P(None, None, "cam"),
        P("pts", "cam"),
        P("pts", "cam"),
    )
    out_specs = (P(None, "cam"), P(None, "cam"))
    body = functools.partial(per_device, mesh.shape["cam"], mesh.shape["pts"])
    return jax.shard_map(body, mesh=mesh, in_specs=in_specs, out_specs=out_specs, check_vma=False)
```

time: 781 us -> 96.5 us (0.12); the launches traced: 765 us -> 96.3 us
  blocking collectives: 337 us -> 0 us
  waiting for transfers between devices: 224 us -> 0 us
  Pallas kernels: 0 us -> 90.6 us
  other arithmetic: 82 us -> 0 us
  local copies, waits for them, and re-layouts: 71.4 us -> 5.07 us
  matrix products: 29.6 us -> 0 us
  between operations: 20.9 us -> 0.64 us
    psum x8 -> x0, blocking collectives: 337 us -> none  [the longest x3 177 us: per_device(): lax.psum(point_part.astype(jnp.bfloat16), 'cam').astype(jnp.float32)]
    psum x3 -> x0, waiting for transfers between devices: 224 us -> none  [per_device(): lax.psum(camera_cols(cam_part).astype(jnp.bfloat16), 'pts')]
    pallas_call x0 -> x1, Pallas kernels: none -> 90.6 us  [per_device(): pl.pallas_call(functools.partial(kernel, n_cam, n_pts), out_shape=(jax.Sh...]
    unnamed x6 -> x0, other arithmetic: 49.2 us -> none
    reshape x10 -> x0, local copies, waits for them, and re-layouts: 37.7 us -> none  [the longest x1 35.9 us: per_device(): blocks = coupling.reshape(tiles_here, 144, slot_count, 192)]
    dot_general x6 -> x0, matrix products: 29.6 us -> none  [the longest x3 27.4 us: per_device(): jnp.einsum('tckp,tkc->tp', blocks, dir_rows, preferred_element_type=jnp.f...]
    reduce_sum x14 -> x0, other arithmetic: 26.9 us -> none  [the longest x3 10 us: per_device(): precond_res = jnp.sum(precond * residual[None, :, :], axis=1)]
    dot_general x9 -> x0, local copies, waits for them, and re-layouts: 12.9 us -> none  [the longest x3 12.3 us: per_device(): jnp.einsum('tckp,tp->tkc', blocks, point_tiles(solved), preferred_element...]
  transfers between devices with their start and end apart: 3 -> 0, of which waited for: 3 -> 0; matrix products, arithmetic and copies ran while one was open for 1% -> 0% of each run, Pallas kernels for 0% -> 0%
where the time goes in v2:
time: 96.5 us; the launch traced here: 96.3 us
  Pallas kernels  90.6 us (94%)
  local copies, waits for them, and re-layouts  5.07 us (5%)
    pallas_call x1, Pallas kernels, per_device(): pl.pallas_call(functools.partial(kernel, n_cam, n_pts), out_shape=(jax.Sh...  90.6 us
    unnamed x8, local copies, waits for them, and re-layouts  5.07 us

profile of v2, /device:TPU:1, one launch (start us, length us, event | category | flops | bytes accessed | tf_op | source)
XLA Modules:
  0.0 96.3 jit_solution(11830152253802472773)
XLA Ops:
  0.6 0.8 copy.9.idx_ref
  1.4 0.7 copy.10.count_ref
  2.1 0.0 copy-start
  2.1 1.0 %copy-done = f32[9,8192]{1,0:T(8,128)S(1)} copy-done((f32[9,8192]{1,0:T(8,128)S(1)}, f32[9,8192]{1,0:T(8,128)}, u32[]{:S(2)}) %copy-start) | copy-done | bytes 294936
  3.2 0.0 copy-start.1
  3.2 0.9 copy-done.1
  4.1 90.6 %shard_map.86 = (f32[9,8192]{1,0:T(8,128)S(1)}, f32[9,8192]{1,0:T(8,128)S(1)}) custom-call(s32[64,4]{1,0:T(8,128)S(1)} %copy.9.idx_ref, s32[64,1]{1,0:T(8,128)S(1)} %copy.10.count_ref, f32[9,8192]{1,0:T(8,128)S(1)} %copy-done, f32[3,3,4096]{2,1,0:T(4,128)S(1)} %copy-done.1, f32[9,9,8192]{2,1,0:T(8,128)} %cam_hbm.1, f32[9,9,8192]{2,1,0:T(8,128)} %pre_hbm.1, ...), custom_call_target="tpu_custom_call" | custom-call | tf_op jit(solution)/shard_map/pallas_call | solution.py:448
  94.7 0.8 copy.13
  95.5 0.8 copy.14
Async XLA Ops:
  2.1 1.0 %copy-start = (f32[9,8192]{1,0:T(8,128)S(1)}, f32[9,8192]{1,0:T(8,128)}, u32[]{:S(2)}) copy-start(f32[9,8192]{1,0:T(8,128)} %rhs_hbm.1) | copy-start | bytes 884740
  3.2 0.9 copy-start.1

commit v3 on v2

--- a/solution.py
+++ b/solution.py
@@ -12,6 +12,8 @@
 BF16 = jnp.bfloat16
 CHUNKS = 16
 HALVES = 2
+UNROLL = 8
+GROUPS = 3
 MESH = pl.DeviceIdType.MESH
 
 
@@ -28,12 +30,12 @@
     idx_ref, count_ref, rhs_hbm, inv_hbm, cam_hbm, pre_hbm, blk_hbm,
     sol_out, res_out,
     blk, cam_nat, pre_nat, rhs_nat, inv_nat, cam_d, pre_d, inv_d,
-    r_ref, z_ref, d_ref, s_ref, q_ref, cz_ref,
+    z_first, r_ref, z_ref, d_ref, s_ref, q_ref, cz_ref,
     pick, place, mask, fold, fold_t, group,
     gath, rows, mid, contrib, even, odd,
-    p_send, p_recv, z_all, t_send, t_recv, dots_c, dots_p, out_nat,
+    p_send, p_recv, z_all, t_send, t_recv, w_all, dots_c, dots_p,
     blk_sem, cam_sem, pre_sem, rhs_sem, inv_sem,
-    ps_s, ps_r, z_s, z_r, t_s, t_r, dc_s, dc_r, dp_s, dp_r, so_s, so_r, re_s, re_r,
+    ps_s, ps_r, z_sem, t_s, t_r, w_s, w_r, dc_s, dc_r, dp_s, dp_r, out_sem,
 ):
     me_c = lax.axis_index("cam")
     me_p = lax.axis_index("pts")
@@ -43,12 +45,16 @@
     per_half = pairs // HALVES
     per_chunk = tiles // CHUNKS
     blocks = place.shape[0]
-    own = rhs_nat.shape[1]
-    lanes_here = pl.ds(pl.multiple_of(me_p * own, own), own)
-
-    pre_copy = pltpu.make_async_copy(pre_hbm.at[:, :, lanes_here], pre_nat, pre_sem)
+    core = lax.rem(me_p, 2)
+    me_z = me_p // 2
+    n_z = n_pts // 2
+    mine = blocks // 2
+    first_block = core * mine
+    lanes_here = pl.ds(pl.multiple_of(first_block * 128, mine * 128), mine * 128)
+
+    pre_copy = pltpu.make_async_copy(pre_hbm, pre_nat, pre_sem)
     cam_copy = pltpu.make_async_copy(cam_hbm.at[:, :, lanes_here], cam_nat, cam_sem)
-    rhs_copy = pltpu.make_async_copy(rhs_hbm.at[:, lanes_here], rhs_nat, rhs_sem)
+    rhs_copy = pltpu.make_async_copy(rhs_hbm, rhs_nat, rhs_sem)
     inv_copy = pltpu.make_async_copy(inv_hbm, inv_nat, inv_sem)
 
     def blk_copy(c):
@@ -129,57 +135,51 @@
 
         lax.fori_loop(1, n_pts, body, 0)
 
-    def part(j):
-        return slice(8 * j, 8 * j + 8)
-
-    def to_dense(src, dst):
-        for b in range(8):
-            dst[pl.ds(b, 9, stride=8), :] = src[:, 128 * b : 128 * b + 128]
-
-    def to_dense_blocks(src, dst):
-        def body(i, carry):
-            for b in range(8):
-                dst[i, pl.ds(b, 9, stride=8), :] = src[i, :, 128 * b : 128 * b + 128]
+    def swap(src, dst, ssem, rsem):
+        return pltpu.make_async_remote_copy(
+            src_ref=src, dst_ref=dst, send_sem=ssem, recv_sem=rsem,
+            device_id=(me_c, me_z * 2 + 1 - core), device_id_type=MESH,
+        )
+
+    def z_peer(k):
+        return lax.rem(me_z + k, n_z)
+
+    def along_z(k, slot, src, dst, ssem, rsem):
+        return pltpu.make_async_remote_copy(
+            src_ref=src, dst_ref=dst(slot), send_sem=ssem.at[k], recv_sem=rsem.at[slot],
+            device_id=(me_c, z_peer(k) * 2 + core), device_id_type=MESH,
+        )
+
+    def at_rows(j, step):
+        return pl.ds(pl.multiple_of(j * mine + step * 8, 8), 8)
+
+    def to_dense_blocks(src, start, dst):
+        def body(b, carry):
+            lanes = pl.ds(pl.multiple_of((start + b) * 128, 128), 128)
+            for i in range(9):
+                dst[i, pl.ds(b, 9, stride=mine), :] = src[i, :, lanes]
             return carry
 
-        lax.fori_loop(0, 9, body, 0)
-
-    def apply_block(mat, vec):
-        out = []
-        for i in range(9):
-            total = mat[i, part(0), :] * vec[0]
-            for j in range(1, 9):
-                total = total + mat[i, part(j), :] * vec[j]
-            out.append(total)
-        return out
-
-    def precondition(r):
-        z = apply_block(pre_d, r)
-        gamma = r[0] * z[0]
+        lax.fori_loop(0, mine, body, 0)
+
+    def apply_row(mat, vec, i, step):
+        total = mat[i, at_rows(0, step), :] * vec[0]
         for j in range(1, 9):
-            gamma = gamma + r[j] * z[j]
-        for j in range(9):
-            z_ref[part(j), :] = z[j]
-            z_all[me_p, :, 128 * j : 128 * j + 128] = z[j].astype(BF16)
-        return gamma
-
-    z_args = (lambda peer: z_all.at[me_p], lambda slot: z_all.at[slot], z_s, z_r)
-
-    rhs_copy.wait()
-    to_dense(rhs_nat, r_ref)
-    pre_copy.wait()
-    to_dense_blocks(pre_nat, pre_d)
-    gamma = precondition([r_ref[part(j), :] for j in range(9)])
-    pl.semaphore_wait(barrier, n_cam + n_pts - 2)
-    start_pts(*z_args)
+            total = total + mat[i, at_rows(j, step), :] * vec[j]
+        return total
+
+    z_swap = swap(z_all.at[core], z_all.at[core], z_sem.at[0], z_sem.at[1])
 
     index = idx_ref[...]
-    used = iota((tiles, 4), 1) < count_ref[...]
+    used = iota((4, tiles), 0) < count_ref[...]
     spread = one_hot(iota((slots, tiles), 0) // 4 == iota((slots, tiles), 1))
     here = iota((slots, 4), 1) == lax.rem(iota((slots, 4), 0), 4)
 
     def column(value):
-        wide = jnp.dot(spread, value.astype(F32).astype(BF16), preferred_element_type=F32)
+        wide = lax.dot_general(
+            spread, value.astype(F32).astype(BF16), (((1,), (1,)), ((), ())),
+            preferred_element_type=F32,
+        )
         return jnp.sum(jnp.where(here, wide, 0.0), axis=1, keepdims=True)
 
     chosen = jnp.where(
@@ -199,18 +199,23 @@
     group[...] = one_hot(
         (col // 8 == lax.rem(row, per_half)) & (lax.rem(col, 8) // 4 == row // per_half)
     )
-    inv_copy.wait()
-
-    def inv_dense(b, carry):
-        for i in range(3):
-            inv_d[i, pl.ds(b, 3, stride=pairs), :] = inv_nat[
-                i, :, pl.ds(pl.multiple_of(b * 128, 128), 128)
-            ]
+
+    rhs_copy.wait()
+    pre_copy.wait()
+
+    def first(b, carry):
+        lanes = pl.ds(pl.multiple_of(b * 128, 128), 128)
+        total = pre_nat[0, :, lanes] * rhs_nat[pl.ds(0, 1), lanes]
+        for j in range(1, 9):
+            total = total + pre_nat[j, :, lanes] * rhs_nat[pl.ds(j, 1), lanes]
+        z_first[pl.ds(b, 9, stride=blocks), :] = total
         return carry
 
-    lax.fori_loop(0, pairs, inv_dense, 0, unroll=4)
-    cam_copy.wait()
-    to_dense_blocks(cam_nat, cam_d)
+    lax.fori_loop(0, blocks, first, 0, unroll=2)
+    for j in range(9):
+        for o in range(2):
+            at = j * blocks + o * mine
+            z_all[o, :, 128 * j : 128 * j + 128] = z_first[at : at + mine, :].astype(BF16)
 
     row8 = iota((8, 768), 0)
     diag = iota((8, 768), 1) // 192 == lax.rem(row8, 4)
@@ -223,7 +228,8 @@
     for it in range(ITERS):
         last = it + 1 == ITERS
         parity = it % 2
-        wait_pts(*z_args)
+        if it > 0:
+            z_swap.wait()
         for j in range(9):
             wide = z_all[:, :, 128 * j : 128 * j + 128].astype(F32).reshape(blocks, 128)
             picked = jnp.dot(pick[...], wide.astype(BF16), preferred_element_type=F32)
@@ -260,13 +266,13 @@
                 lax.fori_loop(h * some, (h + 1) * some, forward_chunk, 0)
             else:
 
-                def forward_four(c, carry):
-                    for k in range(4):
-                        forward(4 * c + k, h)
+                def forward_some(c, carry):
+                    for k in range(UNROLL):
+                        forward(UNROLL * c + k, h)
                     return carry
 
-                some = per_half // 4
-                lax.fori_loop(h * some, (h + 1) * some, forward_four, 0)
+                some = per_half // UNROLL
+                lax.fori_loop(h * some, (h + 1) * some, forward_some, 0)
             full = mid[...]
             high = full.astype(BF16)
             low = (full - high.astype(F32)).astype(BF16)
@@ -277,15 +283,46 @@
             p_send[h] = jnp.where(
                 first_tile, summed[:per_half], pltpu.roll(summed[per_half:], 64, 1)
             ).astype(BF16)
+            if it == 0 and h == 0:
+                pl.semaphore_wait(barrier, n_cam + n_pts - 2)
             start_cam(*p_args(h))
 
-        z = [z_ref[part(j), :] for j in range(9)]
-        cz = apply_block(cam_d, z)
-        curve = z[0] * cz[0]
-        for j in range(1, 9):
-            curve = curve + z[j] * cz[j]
-        for j in range(9):
-            cz_ref[part(j), :] = cz[j]
+        if it == 0:
+
+            def inv_dense(b, carry):
+                for i in range(3):
+                    inv_d[i, pl.ds(b, 3, stride=pairs), :] = inv_nat[
+                        i, :, pl.ds(pl.multiple_of(b * 128, 128), 128)
+                    ]
+                return carry
+
+            inv_copy.wait()
+            lax.fori_loop(0, pairs, inv_dense, 0, unroll=4)
+            for j in range(9):
+                rows_j = pl.ds(pl.multiple_of(j * blocks + first_block, 8), mine)
+                z_ref[j * mine : (j + 1) * mine, :] = z_first[rows_j, :]
+
+            def rhs_dense(b, carry):
+                lanes = pl.ds(pl.multiple_of((first_block + b) * 128, 128), 128)
+                r_ref[pl.ds(b, 9, stride=mine), :] = rhs_nat[:, lanes]
+                return carry
+
+            lax.fori_loop(0, mine, rhs_dense, 0, unroll=4)
+            cam_copy.wait()
+            to_dense_blocks(cam_nat, 0, cam_d)
+
+        def shares(step, carry):
+            gamma, curve = carry
+            z = [z_ref[at_rows(j, step), :] for j in range(9)]
+            for i in range(9):
+                cz = apply_row(cam_d, z, i, step)
+                cz_ref[at_rows(i, step), :] = cz
+                curve = curve + z[i] * cz
+                gamma = gamma + z[i] * r_ref[at_rows(i, step), :]
+            return gamma, curve
+
+        zero = jnp.zeros((8, 128), F32)
+        gamma, curve = lax.fori_loop(0, mine // 8, shares, (zero, zero))
         dots_c[parity, me_c, 0:1, :] = jnp.sum(gamma, axis=0, keepdims=True)
         dots_c[parity, me_c, 1:2, :] = jnp.sum(curve, axis=0, keepdims=True)
         dc_args = (
@@ -337,42 +374,68 @@
                 total = dots_c[parity, 0]
                 for k in range(1, n_cam):
                     total = total + dots_c[parity, k]
-                dots_p[me_p, 0:2, :] = total[0:2]
-                dots_p[me_p, 2:3, :] = jnp.sum(energy, axis=0, keepdims=True)
+                dots_p[parity, me_p, 0:2, :] = total[0:2]
+                dots_p[parity, me_p, 2:3, :] = jnp.sum(energy, axis=0, keepdims=True)
+                dots_p[parity, me_p, 3:4, :] = jnp.sum(energy, axis=0, keepdims=True)
                 dp_args = (
-                    lambda peer: dots_p.at[me_p],
-                    lambda slot: dots_p.at[slot],
+                    lambda peer: dots_p.at[parity, me_p],
+                    lambda slot: dots_p.at[parity, slot],
                     dp_s,
-                    dp_r,
+                    dp_r.at[parity],
                 )
                 start_pts(*dp_args)
 
-            def backward_four(c, carry):
-                for k in range(4):
-                    backward(4 * c + k)
+            def backward_some(c, carry):
+                for k in range(UNROLL):
+                    backward(UNROLL * c + k)
                 return carry
 
-            some = per_half // 4
-            lax.fori_loop(h * some, (h + 1) * some, backward_four, 0)
+            some = per_half // UNROLL
+            lax.fori_loop(h * some, (h + 1) * some, backward_some, 0)
 
         contrib_half = contrib[...].astype(BF16)
-        for j in range(9):
-            lanes = slice(j * 128, (j + 1) * 128)
-            wide = jnp.dot(contrib_half, fold_t[:, lanes], preferred_element_type=F32)
-            wide = (wide * mask[...]).astype(BF16)
-            put = jnp.dot(place[...], wide, preferred_element_type=F32)
-            for o in range(n_pts):
-                t_send[o, :, lanes] = put[o * 8 : (o + 1) * 8, :].astype(BF16)
-        t_args = (lambda peer: t_send.at[peer], lambda slot: t_recv.at[slot], t_s, t_r)
-        start_pts(*t_args)
+        t_swaps = []
+        for g in range(GROUPS):
+            for jj in range(9 // GROUPS):
+                j = g * (9 // GROUPS) + jj
+                lanes = slice(j * 128, (j + 1) * 128)
+                wide = jnp.dot(contrib_half, fold_t[:, lanes], preferred_element_type=F32)
+                wide = (wide * mask[...]).astype(BF16)
+                put = jnp.dot(place[...], wide, preferred_element_type=F32)
+                for o in range(2):
+                    t_send[g, o, :, jj * 128 : (jj + 1) * 128] = put[
+                        o * mine : (o + 1) * mine, :
+                    ].astype(BF16)
+            t_swaps.append(swap(t_send.at[g, 1 - core], t_recv.at[g], t_s.at[g], t_r.at[g]))
+            t_swaps[g].start()
+
+        def w_args(g):
+            return (
+                w_all.at[parity, g, me_z],
+                lambda slot: w_all.at[parity, g, slot],
+                w_s.at[g],
+                w_r.at[parity, g],
+            )
+
+        for g in range(GROUPS):
+            t_swaps[g].wait()
+            w_all[parity, g, me_z] = (
+                t_send[g, core].astype(F32) + t_recv[g].astype(F32)
+            ).astype(BF16)
+            for k in range(1, n_z):
+                along_z(k, me_z, *w_args(g)).start()
+        if it == 0:
+            to_dense_blocks(pre_nat, first_block, pre_d)
 
         wait_pts(*dp_args)
-        total = dots_p[0, 0:3]
+        total = dots_p[parity, 0]
         for k in range(1, n_pts):
-            total = total + dots_p[k, 0:3]
+            total = total + dots_p[parity, k]
+        energy_now = jnp.sum(total[2:3], axis=1, keepdims=True)
+        total = dots_p[parity, 0] + dots_p[parity, 1]
         total = jnp.sum(total, axis=1, keepdims=True)
         gamma_now = total[0:1]
-        curve_now = total[1:2] - total[2:3]
+        curve_now = total[1:2] - energy_now
         if it == 0:
             alpha = gamma_now / curve_now
         else:
@@ -381,70 +444,101 @@
             beta_all = jnp.broadcast_to(beta, (8, 128))
         gamma_old, alpha_old = gamma_now, alpha
         alpha_all = jnp.broadcast_to(alpha, (8, 128))
-        for j in range(9):
-            if it == 0:
-                d = z[j]
+
+        def early(step, carry):
+            for j in range(9):
+                at_j = at_rows(j, step)
+                d = z_ref[at_j, :]
+                q = cz_ref[at_j, :]
+                if it > 0:
+                    d = d + beta_all * d_ref[at_j, :]
+                    q = q + beta_all * q_ref[at_j, :]
                 s = alpha_all * d
-                q = cz[j]
-            else:
-                d = z_ref[part(j), :] + beta_all * d_ref[part(j), :]
-                s = s_ref[part(j), :] + alpha_all * d
-                q = cz_ref[part(j), :] + beta_all * q_ref[part(j), :]
-            d_ref[part(j), :] = d
-            s_ref[part(j), :] = s
-            q_ref[part(j), :] = q
-
-        def to_native(src, which, out):
-            for b in range(8):
-                out_nat[which, :, 128 * b : 128 * b + 128] = src[pl.ds(b, 9, stride=8), :]
-            out[:, lanes_here] = out_nat[which]
-
-        def out_args(which, out, ssem, rsem):
-            return (
-                lambda peer: out_nat.at[which],
-                lambda slot: out.at[:, pl.ds(pl.multiple_of(slot * own, own), own)],
-                ssem,
-                rsem,
-            )
+                if it > 0:
+                    s = s_ref[at_j, :] + s
+                if not last:
+                    d_ref[at_j, :] = d
+                q_ref[at_j, :] = q
+                s_ref[at_j, :] = s
+            return carry
+
+        lax.fori_loop(0, mine // 8, early, 0)
+
+        def to_native(src, out):
+            def body(b, carry):
+                lanes = pl.ds(pl.multiple_of((first_block + b) * 128, 128), 128)
+                out[:, lanes] = src[pl.ds(b, 9, stride=mine), :]
+                return carry
+
+            lax.fori_loop(0, mine, body, 0, unroll=4)
+
+        def out_swap(which, out):
+            half = out.at[:, lanes_here]
+            return swap(half, half, out_sem.at[which, 0], out_sem.at[which, 1])
 
         if last:
-            to_native(s_ref, 0, sol_out)
-            start_pts(*out_args(0, sol_out, so_s, so_r))
-
-        wait_pts(*t_args)
-        r = []
-        for j in range(9):
-            lanes = slice(j * 128, (j + 1) * 128)
-            total = t_send[me_p, :, lanes].astype(F32)
-            for k in range(1, n_pts):
-                total = total + t_recv[pts_peer(k), :, lanes].astype(F32)
-            q = q_ref[part(j), :] - total
-            q_ref[part(j), :] = q
-            value = r_ref[part(j), :] - alpha_all * q
-            r_ref[part(j), :] = value
-            r.append(value)
+            to_native(s_ref, sol_out)
+            out_swap(0, sol_out).start()
+
+        for g in range(GROUPS):
+            for k in range(1, n_z):
+                copy = along_z(k, z_peer(k), *w_args(g))
+                copy.wait_recv()
+                copy.wait_send()
+
+        def late(step, carry):
+            r = []
+            for j in range(9):
+                g, jj = j // (9 // GROUPS), j % (9 // GROUPS)
+                here_j = pl.ds(pl.multiple_of(step * 16, 16), 16)
+                term = w_all[parity, g, 0, here_j, jj * 128 : (jj + 1) * 128].astype(F32)
+                for k in range(1, n_z):
+                    term = term + w_all[
+                        parity, g, k, here_j, jj * 128 : (jj + 1) * 128
+                    ].astype(F32)
+                rr = []
+                for e in range(2):
+                    at_e = at_rows(j, 2 * step + e)
+                    q = q_ref[at_e, :] - term[8 * e : 8 * e + 8]
+                    q_ref[at_e, :] = q
+                    value = r_ref[at_e, :] - alpha_all * q
+                    r_ref[at_e, :] = value
+                    rr.append(value)
+                r.append(rr)
+            if not last:
+                for i in range(9):
+                    zz = []
+                    for e in range(2):
+                        z = apply_row(pre_d, [r[j][e] for j in range(9)], i, 2 * step + e)
+                        z_ref[at_rows(i, 2 * step + e), :] = z
+                        zz.append(z)
+                    z_all[
+                        core, pl.ds(pl.multiple_of(step * 16, 16), 16), 128 * i : 128 * i + 128
+                    ] = jnp.concatenate(zz, axis=0).astype(BF16)
+            return carry
+
+        lax.fori_loop(0, mine // 16, late, 0)
         if not last:
-            gamma = precondition(r)
-            start_pts(*z_args)
+            z_swap.start()
         else:
-            to_native(r_ref, 1, res_out)
-            start_pts(*out_args(1, res_out, re_s, re_r))
-            wait_pts(*out_args(0, sol_out, so_s, so_r))
-            wait_pts(*out_args(1, res_out, re_s, re_r))
+            to_native(r_ref, res_out)
+            out_swap(1, res_out).start()
+            out_swap(0, sol_out).wait()
+            out_swap(1, res_out).wait()
 
 
 def per_device(n_cam, n_pts, rhs, cam_block, coupling, point_inverse, precond, tile_index, tile_count):
     tiles, slots = tile_index.shape
     cams = rhs.shape[1]
     blocks = cams // 128
-    here = cams // n_pts
+    mine = blocks // 2
     pairs = tiles * slots
     half = tiles // 2 // HALVES
-    vec = pltpu.VMEM((72, 128), F32)
+    vec = pltpu.VMEM((9 * mine, 128), F32)
     whole = pl.BlockSpec(memory_space=pltpu.VMEM)
-    hbm = pl.BlockSpec(memory_space=pl.ANY)
+    hbm = pl.BlockSpec(memory_space=pltpu.HBM)
     dma = pltpu.SemaphoreType.DMA
-    slab = pltpu.VMEM((n_pts, 8, 9 * 128), BF16)
+    group = 9 // GROUPS * 128
     return pl.pallas_call(
         functools.partial(kernel, n_cam, n_pts),
         out_shape=(jax.ShapeDtypeStruct(rhs.shape, F32), jax.ShapeDtypeStruct(rhs.shape, F32)),
@@ -452,13 +546,14 @@
         out_specs=(whole, whole),
         scratch_shapes=[
             pltpu.VMEM(coupling.shape, BF16),
-            pltpu.VMEM((9, 9, here), F32),
-            pltpu.VMEM((9, 9, here), F32),
-            pltpu.VMEM((9, here), F32),
+            pltpu.VMEM((9, 9, mine * 128), F32),
+            pltpu.VMEM(precond.shape, F32),
+            pltpu.VMEM(rhs.shape, F32),
             pltpu.VMEM(point_inverse.shape, F32),
-            pltpu.VMEM((9, 72, 128), F32),
-            pltpu.VMEM((9, 72, 128), F32),
+            pltpu.VMEM((9, 9 * mine, 128), F32),
+            pltpu.VMEM((9, 9 * mine, 128), F32),
             pltpu.VMEM((3, 3 * tiles // 2, 128), F32),
+            pltpu.VMEM((9 * blocks, 128), F32),
             vec, vec, vec, vec, vec, vec,
             pltpu.VMEM((pairs, blocks), BF16),
             pltpu.VMEM((blocks, pairs), BF16),
@@ -474,23 +569,25 @@
             pltpu.VMEM((tiles // 2, 384), F32),
             pltpu.VMEM((HALVES, half, 384), BF16),
             pltpu.VMEM((2, HALVES, n_cam, half, 384), BF16),
-            slab, slab, slab,
+            pltpu.VMEM((2, mine, 9 * 128), BF16),
+            pltpu.VMEM((GROUPS, 2, mine, group), BF16),
+            pltpu.VMEM((GROUPS, mine, group), BF16),
+            pltpu.VMEM((2, GROUPS, n_pts // 2, mine, group), BF16),
             pltpu.VMEM((2, n_cam, 2, 128), F32),
-            pltpu.VMEM((n_pts, 4, 128), F32),
-            pltpu.VMEM((2, 9, here), F32),
+            pltpu.VMEM((2, n_pts, 4, 128), F32),
             dma((CHUNKS,)), dma, dma, dma, dma,
             dma((HALVES, n_cam)), dma((2, HALVES, n_cam)),
-            dma((n_pts,)), dma((n_pts,)),
-            dma((n_pts,)), dma((n_pts,)),
+            dma((2,)),
+            dma((GROUPS,)), dma((GROUPS,)),
+            dma((GROUPS, n_pts // 2)), dma((2, GROUPS, n_pts // 2)),
             dma((n_cam,)), dma((2, n_cam)),
-            dma((n_pts,)), dma((n_pts,)),
-            dma((n_pts,)), dma((n_pts,)),
-            dma((n_pts,)), dma((n_pts,)),
+            dma((n_pts,)), dma((2, n_pts)),
+            dma((2, 2)),
         ],
         compiler_params=pltpu.CompilerParams(
-            collective_id=0, has_side_effects=True, vmem_limit_bytes=48 * 2**20
+            collective_id=0, has_side_effects=True, vmem_limit_bytes=56 * 2**20
         ),
-    )(tile_index, tile_count, rhs, point_inverse, cam_block, precond, coupling)
+    )(tile_index.T, tile_count.T, rhs, point_inverse, cam_block, precond, coupling)
 
 
 def solution(mesh):

time: 96.5 us -> 84.9 us (0.88)
  Pallas kernels: 90.6 us -> 80.3 us
  local copies, waits for them, and re-layouts: 5.07 us -> 3.74 us
    pallas_call x1, Pallas kernels: 90.6 us -> 80.3 us  [per_device(): pl.pallas_call(functools.partial(kernel, n_cam, n_pts), out_shape=(jax.Sh...]
    unnamed x8 -> x2, local copies, waits for them, and re-layouts: 5.07 us -> 3.74 us
where the time goes in v3:
time: 84.9 us; the launch traced here: 84.7 us
  Pallas kernels  80.3 us (95%)
  local copies, waits for them, and re-layouts  3.74 us (4%)
    pallas_call x1, Pallas kernels, per_device(): pl.pallas_call(functools.partial(kernel, n_cam, n_pts), out_shape=(jax.Sh...  80.3 us
    unnamed x2, local copies, waits for them, and re-layouts  3.74 us

profile of v3, /device:TPU:1, one launch (start us, length us, event | category | flops | bytes accessed | tf_op | source)
XLA Modules:
  0.0 84.7 jit_solution(8412269016446910703)
XLA Ops:
  0.6 80.3 %shard_map.86 = (f32[9,8192]{1,0:T(8,128)}, f32[9,8192]{1,0:T(8,128)}) custom-call(s32[4,64]{1,0:T(4,128)} %bitcast.2, s32[1,64]{1,0:T(1,128)} %bitcast.3, f32[9,8192]{1,0:T(8,128)} %rhs_hbm.1, f32[3,3,4096]{2,1,0:T(4,128)} %inv_hbm.1, f32[9,9,8192]{2,1,0:T(8,128)} %cam_hbm.1, f32[9,9,8192]{2,1,0:T(8,128)} %pre_hbm.1, bf16[64,144,768]{2,1,0:T(8,128)(2,1)} %blk_hbm.1), custom_call_target="tpu_custom_call" | custom-call | tf_op jit(solution)/shard_map/pallas_call | solution.py:542
  80.9 1.9 %copy.11 = f32[9,8192]{1,0:T(8,128)} copy(f32[9,8192]{1,0:T(8,128)} %get-tuple-element.4) | data formatting | bytes 589824
  82.8 1.9 %copy.12 = f32[9,8192]{1,0:T(8,128)} copy(f32[9,8192]{1,0:T(8,128)} %get-tuple-element.5) | data formatting | bytes 589824

commit v4 on v3

--- a/solution.py
+++ b/solution.py
@@ -11,7 +11,7 @@
 F32 = jnp.float32
 BF16 = jnp.bfloat16
 CHUNKS = 16
-HALVES = 2
+PIECES = 4
 UNROLL = 8
 GROUPS = 3
 MESH = pl.DeviceIdType.MESH
@@ -33,7 +33,7 @@
     z_first, r_ref, z_ref, d_ref, s_ref, q_ref, cz_ref,
     pick, place, mask, fold, fold_t, group,
     gath, rows, mid, contrib, even, odd,
-    p_send, p_recv, z_all, t_send, t_recv, w_all, dots_c, dots_p,
+    p_recv, z_all, t_send, t_recv, w_all, dots_c, dots_p,
     blk_sem, cam_sem, pre_sem, rhs_sem, inv_sem,
     ps_s, ps_r, z_sem, t_s, t_r, w_s, w_r, dc_s, dc_r, dp_s, dp_r, out_sem,
 ):
@@ -42,7 +42,7 @@
     tiles = blk.shape[0]
     pairs = tiles // 2
     slots = 4 * tiles
-    per_half = pairs // HALVES
+    per_piece = pairs // PIECES
     per_chunk = tiles // CHUNKS
     blocks = place.shape[0]
     core = lax.rem(me_p, 2)
@@ -110,11 +110,16 @@
 
         lax.fori_loop(1, n_cam, body, 0)
 
-    def wait_cam(*args):
+    def arrive_cam(*args):
         def body(k, carry):
-            copy = cam_copy_to(cam_peer(k), cam_peer(k), *args)
-            copy.wait_recv()
-            copy.wait_send()
+            cam_copy_to(cam_peer(k), cam_peer(k), *args).wait_recv()
+            return carry
+
+        lax.fori_loop(1, n_cam, body, 0)
+
+    def left_cam(*args):
+        def body(k, carry):
+            cam_copy_to(cam_peer(k), cam_peer(k), *args).wait_send()
             return carry
 
         lax.fori_loop(1, n_cam, body, 0)
@@ -194,10 +199,10 @@
     fold[...] = one_hot(iota((9 * 128, 144), 1) == (at // 128) * 16 + lax.rem(at, 16))
     at = iota((144, 9 * 128), 1)
     fold_t[...] = one_hot(iota((144, 9 * 128), 0) == (at // 128) * 16 + lax.rem(at, 16))
-    row = iota((2 * per_half, 8 * per_half), 0)
-    col = iota((2 * per_half, 8 * per_half), 1)
+    row = iota((2 * per_piece, 8 * per_piece), 0)
+    col = iota((2 * per_piece, 8 * per_piece), 1)
     group[...] = one_hot(
-        (col // 8 == lax.rem(row, per_half)) & (lax.rem(col, 8) // 4 == row // per_half)
+        (col // 8 == lax.rem(row, per_piece)) & (lax.rem(col, 8) // 4 == row // per_piece)
     )
 
     rhs_copy.wait()
@@ -220,7 +225,7 @@
     row8 = iota((8, 768), 0)
     diag = iota((8, 768), 1) // 192 == lax.rem(row8, 4)
     upper = row8 < 4
-    first_tile = lax.rem(iota((per_half, 384), 1), 128) < 64
+    first_tile = lax.rem(iota((per_piece, 384), 1), 128) < 64
     order = (0, 2, 1)
 
     gamma_old = None
@@ -241,19 +246,19 @@
             one = jnp.dot(left, blk[2 * j], preferred_element_type=F32)
             two = jnp.dot(left, blk[2 * j + 1], preferred_element_type=F32)
             both = jnp.where(diag, jnp.where(upper, one, two), 0.0)
-            mid[pl.ds(pl.multiple_of(8 * (j - h * per_half), 8), 8), :] = (
+            mid[pl.ds(pl.multiple_of(8 * (j - h * per_piece), 8), 8), :] = (
                 both[:, :384] + both[:, 384:]
             )
 
         def p_args(h):
             return (
-                lambda peer: p_send.at[h],
+                lambda peer: p_recv.at[parity, h, me_c],
                 lambda slot: p_recv.at[parity, h, slot],
                 ps_s.at[h],
                 ps_r.at[parity, h],
             )
 
-        for h in range(HALVES):
+        for h in range(PIECES):
             if it == 0:
 
                 def forward_chunk(c, carry):
@@ -262,7 +267,7 @@
                         forward(c * (per_chunk // 2) + k, h)
                     return carry
 
-                some = CHUNKS // HALVES
+                some = CHUNKS // PIECES
                 lax.fori_loop(h * some, (h + 1) * some, forward_chunk, 0)
             else:
 
@@ -271,7 +276,7 @@
                         forward(UNROLL * c + k, h)
                     return carry
 
-                some = per_half // UNROLL
+                some = per_piece // UNROLL
                 lax.fori_loop(h * some, (h + 1) * some, forward_some, 0)
             full = mid[...]
             high = full.astype(BF16)
@@ -280,8 +285,8 @@
                 group[...], low, preferred_element_type=F32
             )
             summed = summed + pltpu.roll(summed, 192, 1)
-            p_send[h] = jnp.where(
-                first_tile, summed[:per_half], pltpu.roll(summed[per_half:], 64, 1)
+            p_recv[parity, h, me_c] = jnp.where(
+                first_tile, summed[:per_piece], pltpu.roll(summed[per_piece:], 64, 1)
             ).astype(BF16)
             if it == 0 and h == 0:
                 pl.semaphore_wait(barrier, n_cam + n_pts - 2)
@@ -345,21 +350,21 @@
             two = lax.dot_general(left, blk[2 * j + 1], contract, preferred_element_type=F32)
             contrib[pl.ds(pl.multiple_of(8 * j, 8), 8), :] = jnp.where(upper[:, :144], one, two)
 
-        energy = jnp.zeros((per_half, 128), F32)
-        for h in range(HALVES):
-            wait_cam(*p_args(h))
-            total = p_send[h].astype(F32)
+        energy = jnp.zeros((per_piece, 128), F32)
+        for h in range(PIECES):
+            arrive_cam(*p_args(h))
+            total = p_recv[parity, h, 0].astype(F32)
             for k in range(1, n_cam):
-                total = total + p_recv[parity, h, cam_peer(k)].astype(F32)
+                total = total + p_recv[parity, h, k].astype(F32)
             sums = [None] * 3
             for place_i, i in enumerate(order):
                 sums[i] = total[:, 128 * place_i : 128 * place_i + 128]
-            here_h = slice(h * per_half, (h + 1) * per_half)
+            here_h = slice(h * per_piece, (h + 1) * per_piece)
             answers = []
             for i in order:
-                answer = jnp.zeros((per_half, 128), F32)
+                answer = jnp.zeros((per_piece, 128), F32)
                 for j in range(3):
-                    at_j = slice(j * pairs + h * per_half, j * pairs + (h + 1) * per_half)
+                    at_j = slice(j * pairs + h * per_piece, j * pairs + (h + 1) * per_piece)
                     answer = answer + inv_d[i, at_j, :] * sums[j]
                 answer = answer.astype(BF16).astype(F32)
                 energy = energy + answer * sums[i]
@@ -369,8 +374,8 @@
             even[here_h, :] = a + pltpu.roll(a, 192, 1)
             a = pltpu.roll(jnp.where(first_tile, 0.0, answer), 320, 1)
             odd[here_h, :] = a + pltpu.roll(a, 192, 1)
-            if h + 1 == HALVES:
-                wait_cam(*dc_args)
+            if h + 1 == PIECES:
+                arrive_cam(*dc_args)
                 total = dots_c[parity, 0]
                 for k in range(1, n_cam):
                     total = total + dots_c[parity, k]
@@ -390,22 +395,20 @@
                     backward(UNROLL * c + k)
                 return carry
 
-            some = per_half // UNROLL
+            some = per_piece // UNROLL
             lax.fori_loop(h * some, (h + 1) * some, backward_some, 0)
 
         contrib_half = contrib[...].astype(BF16)
+        width = 9 // GROUPS * 128
+        mask_wide = jnp.concatenate([mask[...]] * (9 // GROUPS), axis=1)
         t_swaps = []
         for g in range(GROUPS):
-            for jj in range(9 // GROUPS):
-                j = g * (9 // GROUPS) + jj
-                lanes = slice(j * 128, (j + 1) * 128)
-                wide = jnp.dot(contrib_half, fold_t[:, lanes], preferred_element_type=F32)
-                wide = (wide * mask[...]).astype(BF16)
-                put = jnp.dot(place[...], wide, preferred_element_type=F32)
-                for o in range(2):
-                    t_send[g, o, :, jj * 128 : (jj + 1) * 128] = put[
-                        o * mine : (o + 1) * mine, :
-                    ].astype(BF16)
+            lanes = slice(g * width, (g + 1) * width)
+            wide = jnp.dot(contrib_half, fold_t[:, lanes], preferred_element_type=F32)
+            wide = (wide * mask_wide).astype(BF16)
+            put = jnp.dot(place[...], wide, preferred_element_type=F32)
+            for o in range(2):
+                t_send[g, o] = put[o * mine : (o + 1) * mine, :].astype(BF16)
             t_swaps.append(swap(t_send.at[g, 1 - core], t_recv.at[g], t_s.at[g], t_r.at[g]))
             t_swaps[g].start()
 
@@ -463,6 +466,9 @@
             return carry
 
         lax.fori_loop(0, mine // 8, early, 0)
+        for h in range(PIECES):
+            left_cam(*p_args(h))
+        left_cam(*dc_args)
 
         def to_native(src, out):
             def body(b, carry):
@@ -533,12 +539,14 @@
     blocks = cams // 128
     mine = blocks // 2
     pairs = tiles * slots
-    half = tiles // 2 // HALVES
+    half = tiles // 2 // PIECES
     vec = pltpu.VMEM((9 * mine, 128), F32)
     whole = pl.BlockSpec(memory_space=pltpu.VMEM)
     hbm = pl.BlockSpec(memory_space=pltpu.HBM)
     dma = pltpu.SemaphoreType.DMA
     group = 9 // GROUPS * 128
+    big = (rhs, point_inverse, cam_block, precond, coupling)
+    big = [pltpu.with_memory_space_constraint(x, pltpu.HBM) for x in big]
     return pl.pallas_call(
         functools.partial(kernel, n_cam, n_pts),
         out_shape=(jax.ShapeDtypeStruct(rhs.shape, F32), jax.ShapeDtypeStruct(rhs.shape, F32)),
@@ -567,8 +575,7 @@
             pltpu.VMEM((pairs, 144), F32),
             pltpu.VMEM((tiles // 2, 384), F32),
             pltpu.VMEM((tiles // 2, 384), F32),
-            pltpu.VMEM((HALVES, half, 384), BF16),
-            pltpu.VMEM((2, HALVES, n_cam, half, 384), BF16),
+            pltpu.VMEM((2, PIECES, n_cam, half, 384), BF16),
             pltpu.VMEM((2, mine, 9 * 128), BF16),
             pltpu.VMEM((GROUPS, 2, mine, group), BF16),
             pltpu.VMEM((GROUPS, mine, group), BF16),
@@ -576,7 +583,7 @@
             pltpu.VMEM((2, n_cam, 2, 128), F32),
             pltpu.VMEM((2, n_pts, 4, 128), F32),
             dma((CHUNKS,)), dma, dma, dma, dma,
-            dma((HALVES, n_cam)), dma((2, HALVES, n_cam)),
+            dma((PIECES, n_cam)), dma((2, PIECES, n_cam)),
             dma((2,)),
             dma((GROUPS,)), dma((GROUPS,)),
             dma((GROUPS, n_pts // 2)), dma((2, GROUPS, n_pts // 2)),
@@ -585,9 +592,9 @@
             dma((2, 2)),
         ],
         compiler_params=pltpu.CompilerParams(
-            collective_id=0, has_side_effects=True, vmem_limit_bytes=56 * 2**20
+            collective_id=0, has_side_effects=True, vmem_limit_bytes=52 * 2**20
         ),
-    )(tile_index.T, tile_count.T, rhs, point_inverse, cam_block, precond, coupling)
+    )(tile_index.T, tile_count.T, *big)
 
 
 def solution(mesh):

time: 84.9 us -> 79.2 us (0.933)
  Pallas kernels: 80.3 us -> 75.4 us
    pallas_call x1, Pallas kernels: 80.3 us -> 75.4 us  [per_device(): pl.pallas_call(functools.partial(kernel, n_cam, n_pts), out_shape=(jax.Sh...]
    unnamed x2 -> x6, local copies, waits for them, and re-layouts: 3.74 us -> 2.92 us
where the time goes in v4:
time: 79.2 us; the launch traced here: 79 us
  Pallas kernels  75.4 us (95%)
  local copies, waits for them, and re-layouts  2.92 us (4%)
    pallas_call x1, Pallas kernels, per_device(): pl.pallas_call(functools.partial(kernel, n_cam, n_pts), out_shape=(jax.Sh...  75.4 us
    unnamed x6, local copies, waits for them, and re-layouts  2.92 us

profile of v4, /device:TPU:1, one launch (start us, length us, event | category | flops | bytes accessed | tf_op | source)
XLA Modules:
  0.0 79.0 jit_solution(1697175478187648384)
XLA Ops:
  0.6 0.0 copy-start
  0.6 0.7 copy-done
  1.3 0.0 copy-start.1
  1.3 0.7 copy-done.1
  2.0 75.4 %shard_map.86 = (f32[9,8192]{1,0:T(8,128)S(1)}, f32[9,8192]{1,0:T(8,128)S(1)}) custom-call(s32[4,64]{1,0:T(4,128)S(1)} %bitcast.2, s32[1,64]{1,0:T(1,128)S(1)} %bitcast.3, f32[9,8192]{1,0:T(8,128)} %rhs_hbm.1, f32[3,3,4096]{2,1,0:T(4,128)} %inv_hbm.1, f32[9,9,8192]{2,1,0:T(8,128)} %cam_hbm.1, f32[9,9,8192]{2,1,0:T(8,128)} %pre_hbm.1, ...), custom_call_target="tpu_custom_call" | custom-call | tf_op jit(solution)/shard_map/pallas_call | solution.py:550
  77.4 0.8 %copy.11 = f32[9,8192]{1,0:T(8,128)} copy(f32[9,8192]{1,0:T(8,128)S(1)} %get-tuple-element.4) | data formatting | bytes 589824
  78.2 0.8 %copy.12 = f32[9,8192]{1,0:T(8,128)} copy(f32[9,8192]{1,0:T(8,128)S(1)} %get-tuple-element.5) | data formatting | bytes 589824
Async XLA Ops:
  0.6 0.7 copy-start
  1.3 0.7 copy-start.1

commit v5 on v4

--- a/solution.py
+++ b/solution.py
@@ -27,14 +27,14 @@
 
 def kernel(
     n_cam, n_pts,
-    idx_ref, count_ref, rhs_hbm, inv_hbm, cam_hbm, pre_hbm, blk_hbm,
+    idx_hbm, count_hbm, rhs_hbm, inv_hbm, cam_hbm, pre_hbm, blk_hbm,
     sol_out, res_out,
-    blk, cam_nat, pre_nat, rhs_nat, inv_nat, cam_d, pre_d, inv_d,
+    idx_ref, count_ref, blk, cam_nat, pre_nat, rhs_nat, inv_nat, cam_d, pre_d, inv_d,
     z_first, r_ref, z_ref, d_ref, s_ref, q_ref, cz_ref,
     pick, place, mask, fold, fold_t, group,
-    gath, rows, mid, contrib, even, odd,
+    gath, rows, mid, contrib, contrib_last, wide_ref, even, odd,
     p_recv, z_all, t_send, t_recv, w_all, dots_c, dots_p,
-    blk_sem, cam_sem, pre_sem, rhs_sem, inv_sem,
+    blk_sem, cam_sem, pre_sem, rhs_sem, inv_sem, idx_sem, count_sem,
     ps_s, ps_r, z_sem, t_s, t_r, w_s, w_r, dc_s, dc_r, dp_s, dp_r, out_sem,
 ):
     me_c = lax.axis_index("cam")
@@ -61,6 +61,29 @@
         part = pl.ds(c * per_chunk, per_chunk)
         return pltpu.make_async_copy(blk_hbm.at[part], blk.at[part], blk_sem.at[c])
 
+    barrier = pltpu.get_barrier_semaphore()
+
+    def cam_peer(k):
+        return lax.rem(me_c + k, n_cam)
+
+    def pts_peer(k):
+        return lax.rem(me_p + k, n_pts)
+
+    def greet_cam(k, carry):
+        pl.semaphore_signal(barrier, inc=1, device_id=(cam_peer(k), me_p), device_id_type=MESH)
+        return carry
+
+    def greet_pts(k, carry):
+        pl.semaphore_signal(barrier, inc=1, device_id=(me_c, pts_peer(k)), device_id_type=MESH)
+        return carry
+
+    lax.fori_loop(1, n_cam, greet_cam, 0)
+    lax.fori_loop(1, n_pts, greet_pts, 0)
+
+    idx_copy = pltpu.make_async_copy(idx_hbm, idx_ref, idx_sem)
+    count_copy = pltpu.make_async_copy(count_hbm, count_ref, count_sem)
+    idx_copy.start()
+    count_copy.start()
     rhs_copy.start()
     pre_copy.start()
 
@@ -71,25 +94,6 @@
     lax.fori_loop(0, CHUNKS, start_chunk, 0)
     inv_copy.start()
     cam_copy.start()
-
-    barrier = pltpu.get_barrier_semaphore()
-
-    def cam_peer(k):
-        return lax.rem(me_c + k, n_cam)
-
-    def pts_peer(k):
-        return lax.rem(me_p + k, n_pts)
-
-    def greet_cam(k, carry):
-        pl.semaphore_signal(barrier, inc=1, device_id=(cam_peer(k), me_p), device_id_type=MESH)
-        return carry
-
-    def greet_pts(k, carry):
-        pl.semaphore_signal(barrier, inc=1, device_id=(me_c, pts_peer(k)), device_id_type=MESH)
-        return carry
-
-    lax.fori_loop(1, n_cam, greet_cam, 0)
-    lax.fori_loop(1, n_pts, greet_pts, 0)
 
     def cam_copy_to(peer, slot, src, dst, ssem, rsem):
         return pltpu.make_async_remote_copy(
@@ -175,26 +179,6 @@
 
     z_swap = swap(z_all.at[core], z_all.at[core], z_sem.at[0], z_sem.at[1])
 
-    index = idx_ref[...]
-    used = iota((4, tiles), 0) < count_ref[...]
-    spread = one_hot(iota((slots, tiles), 0) // 4 == iota((slots, tiles), 1))
-    here = iota((slots, 4), 1) == lax.rem(iota((slots, 4), 0), 4)
-
-    def column(value):
-        wide = lax.dot_general(
-            spread, value.astype(F32).astype(BF16), (((1,), (1,)), ((), ())),
-            preferred_element_type=F32,
-        )
-        return jnp.sum(jnp.where(here, wide, 0.0), axis=1, keepdims=True)
-
-    chosen = jnp.where(
-        iota((slots, blocks), 1).astype(F32) == column(jnp.where(used, index // 8, -1)), 1.0, 0.0
-    )
-    pick[...] = chosen.astype(BF16)
-    place[...] = jnp.transpose(chosen).astype(BF16)
-    mask[...] = jnp.where(
-        (iota((slots, 128), 1) // 16).astype(F32) == column(lax.rem(index, 8)), 1.0, 0.0
-    )
     at = iota((9 * 128, 144), 0)
     fold[...] = one_hot(iota((9 * 128, 144), 1) == (at // 128) * 16 + lax.rem(at, 16))
     at = iota((144, 9 * 128), 1)
@@ -203,6 +187,28 @@
     col = iota((2 * per_piece, 8 * per_piece), 1)
     group[...] = one_hot(
         (col // 8 == lax.rem(row, per_piece)) & (lax.rem(col, 8) // 4 == row // per_piece)
+    )
+    idx_copy.wait()
+    count_copy.wait()
+    index = idx_ref[...]
+    used = iota((4, tiles), 0) < count_ref[...]
+    spread = one_hot(iota((slots, tiles), 0) // 4 == iota((slots, tiles), 1))
+    here = iota((slots, 4), 1) == lax.rem(iota((slots, 4), 0), 4)
+
+    def column(value):
+        wide = lax.dot_general(
+            spread, value.astype(F32).astype(BF16), (((1,), (1,)), ((), ())),
+            preferred_element_type=F32,
+        )
+        return jnp.sum(jnp.where(here, wide, 0.0), axis=1, keepdims=True)
+
+    chosen = jnp.where(
+        iota((slots, blocks), 1).astype(F32) == column(jnp.where(used, index // 8, -1)), 1.0, 0.0
+    )
+    pick[...] = chosen.astype(BF16)
+    place[...] = jnp.transpose(chosen).astype(BF16)
+    mask[...] = jnp.where(
+        (iota((slots, 128), 1) // 16).astype(F32) == column(lax.rem(index, 8)), 1.0, 0.0
     )
 
     rhs_copy.wait()
@@ -338,7 +344,7 @@
         )
         start_cam(*dc_args)
 
-        def backward(j):
+        def backward(j, lines, out, at):
             both = jnp.where(
                 upper[:, :384],
                 jnp.broadcast_to(even[pl.ds(j, 1), :], (8, 384)),
@@ -346,12 +352,25 @@
             )
             left = jnp.where(diag, jnp.concatenate([both, both], axis=1), 0.0).astype(BF16)
             contract = (((1,), (1,)), ((), ()))
-            one = lax.dot_general(left, blk[2 * j], contract, preferred_element_type=F32)
-            two = lax.dot_general(left, blk[2 * j + 1], contract, preferred_element_type=F32)
-            contrib[pl.ds(pl.multiple_of(8 * j, 8), 8), :] = jnp.where(upper[:, :144], one, two)
-
+            one = lax.dot_general(left, blk[2 * j, lines, :], contract, preferred_element_type=F32)
+            two = lax.dot_general(
+                left, blk[2 * j + 1, lines, :], contract, preferred_element_type=F32
+            )
+            out[at, :] = jnp.where(upper[:, : one.shape[1]], one, two)
+
+        width = 9 // GROUPS * 128
+        mask_wide = jnp.concatenate([mask[...]] * (9 // GROUPS), axis=1)
+        early_rows = 8 * per_piece * (PIECES - 1)
         energy = jnp.zeros((per_piece, 128), F32)
         for h in range(PIECES):
+            if h + 1 == PIECES:
+                contrib_half = contrib[0:early_rows, :].astype(BF16)
+                for g in range(GROUPS):
+                    wide = jnp.dot(
+                        contrib_half, fold_t[:, g * width : (g + 1) * width],
+                        preferred_element_type=F32,
+                    )
+                    wide_ref[g, 0:early_rows, :] = (wide * mask_wide[:early_rows]).astype(BF16)
             arrive_cam(*p_args(h))
             total = p_recv[parity, h, 0].astype(F32)
             for k in range(1, n_cam):
@@ -390,27 +409,16 @@
                 )
                 start_pts(*dp_args)
 
-            def backward_some(c, carry):
-                for k in range(UNROLL):
-                    backward(UNROLL * c + k)
-                return carry
-
-            some = per_piece // UNROLL
-            lax.fori_loop(h * some, (h + 1) * some, backward_some, 0)
-
-        contrib_half = contrib[...].astype(BF16)
-        width = 9 // GROUPS * 128
-        mask_wide = jnp.concatenate([mask[...]] * (9 // GROUPS), axis=1)
-        t_swaps = []
-        for g in range(GROUPS):
-            lanes = slice(g * width, (g + 1) * width)
-            wide = jnp.dot(contrib_half, fold_t[:, lanes], preferred_element_type=F32)
-            wide = (wide * mask_wide).astype(BF16)
-            put = jnp.dot(place[...], wide, preferred_element_type=F32)
-            for o in range(2):
-                t_send[g, o] = put[o * mine : (o + 1) * mine, :].astype(BF16)
-            t_swaps.append(swap(t_send.at[g, 1 - core], t_recv.at[g], t_s.at[g], t_r.at[g]))
-            t_swaps[g].start()
+            if h + 1 < PIECES:
+
+                def backward_some(c, carry):
+                    for k in range(UNROLL):
+                        j = UNROLL * c + k
+                        backward(j, slice(0, 144), contrib, pl.ds(pl.multiple_of(8 * j, 8), 8))
+                    return carry
+
+                some = per_piece // UNROLL
+                lax.fori_loop(h * some, (h + 1) * some, backward_some, 0)
 
         def w_args(g):
             return (
@@ -420,13 +428,34 @@
                 w_r.at[parity, g],
             )
 
-        for g in range(GROUPS):
+        def send_along_z(g):
             t_swaps[g].wait()
             w_all[parity, g, me_z] = (
                 t_send[g, core].astype(F32) + t_recv[g].astype(F32)
             ).astype(BF16)
             for k in range(1, n_z):
                 along_z(k, me_z, *w_args(g)).start()
+
+        t_swaps = []
+        lines = 144 // GROUPS
+        for g in range(GROUPS):
+            for k in range(per_piece):
+                backward(
+                    (PIECES - 1) * per_piece + k, slice(g * lines, (g + 1) * lines),
+                    contrib_last.at[g], slice(8 * k, 8 * k + 8),
+                )
+            wide = jnp.dot(
+                contrib_last[g].astype(BF16), fold_t[0:lines, 0:width], preferred_element_type=F32
+            )
+            wide_ref[g, early_rows:, :] = (wide * mask_wide[early_rows:]).astype(BF16)
+            put = jnp.dot(place[...], wide_ref[g], preferred_element_type=F32)
+            for o in range(2):
+                t_send[g, o] = put[o * mine : (o + 1) * mine, :].astype(BF16)
+            t_swaps.append(swap(t_send.at[g, 1 - core], t_recv.at[g], t_s.at[g], t_r.at[g]))
+            t_swaps[g].start()
+            if g > 0:
+                send_along_z(g - 1)
+        send_along_z(GROUPS - 1)
         if it == 0:
             to_dense_blocks(pre_nat, first_block, pre_d)
 
@@ -486,49 +515,61 @@
             to_native(s_ref, sol_out)
             out_swap(0, sol_out).start()
 
-        for g in range(GROUPS):
-            for k in range(1, n_z):
-                copy = along_z(k, z_peer(k), *w_args(g))
-                copy.wait_recv()
-                copy.wait_send()
-
-        def late(step, carry):
-            r = []
-            for j in range(9):
-                g, jj = j // (9 // GROUPS), j % (9 // GROUPS)
-                here_j = pl.ds(pl.multiple_of(step * 16, 16), 16)
-                term = w_all[parity, g, 0, here_j, jj * 128 : (jj + 1) * 128].astype(F32)
+        def late(g, step):
+            some = range(g * (9 // GROUPS), (g + 1) * (9 // GROUPS))
+            here_j = pl.ds(pl.multiple_of(step * 16, 16), 16)
+            r = {}
+            for j in some:
+                lanes = slice((j - some[0]) * 128, (j - some[0] + 1) * 128)
+                term = w_all[parity, g, 0, here_j, lanes].astype(F32)
                 for k in range(1, n_z):
-                    term = term + w_all[
-                        parity, g, k, here_j, jj * 128 : (jj + 1) * 128
-                    ].astype(F32)
-                rr = []
+                    term = term + w_all[parity, g, k, here_j, lanes].astype(F32)
                 for e in range(2):
                     at_e = at_rows(j, 2 * step + e)
                     q = q_ref[at_e, :] - term[8 * e : 8 * e + 8]
                     q_ref[at_e, :] = q
                     value = r_ref[at_e, :] - alpha_all * q
                     r_ref[at_e, :] = value
-                    rr.append(value)
-                r.append(rr)
-            if not last:
-                for i in range(9):
-                    zz = []
-                    for e in range(2):
-                        z = apply_row(pre_d, [r[j][e] for j in range(9)], i, 2 * step + e)
-                        z_ref[at_rows(i, 2 * step + e), :] = z
-                        zz.append(z)
-                    z_all[
-                        core, pl.ds(pl.multiple_of(step * 16, 16), 16), 128 * i : 128 * i + 128
-                    ] = jnp.concatenate(zz, axis=0).astype(BF16)
-            return carry
-
-        lax.fori_loop(0, mine // 16, late, 0)
+                    r[j, e] = value
+            if last:
+                return
+            for i in range(9):
+                zz = []
+                for e in range(2):
+                    z = pre_d[i, at_rows(some[0], 2 * step + e), :] * r[some[0], e]
+                    for j in some[1:]:
+                        z = z + pre_d[i, at_rows(j, 2 * step + e), :] * r[j, e]
+                    if g > 0:
+                        z = z_ref[at_rows(i, 2 * step + e), :] + z
+                    z_ref[at_rows(i, 2 * step + e), :] = z
+                    zz.append(z)
+                if g + 1 == GROUPS:
+                    z_all[core, here_j, 128 * i : 128 * i + 128] = jnp.concatenate(
+                        zz, axis=0
+                    ).astype(BF16)
+
+        for g in range(GROUPS):
+            for k in range(1, n_z):
+                along_z(k, z_peer(k), *w_args(g)).wait_recv()
+
+            def late_step(step, carry):
+                late(g, step)
+                return carry
+
+            lax.fori_loop(0, mine // 16, late_step, 0)
+
+        def left_z():
+            for g in range(GROUPS):
+                for k in range(1, n_z):
+                    along_z(k, z_peer(k), *w_args(g)).wait_send()
+
         if not last:
             z_swap.start()
+            left_z()
         else:
             to_native(r_ref, res_out)
             out_swap(1, res_out).start()
+            left_z()
             out_swap(0, sol_out).wait()
             out_swap(1, res_out).wait()
 
@@ -545,14 +586,16 @@
     hbm = pl.BlockSpec(memory_space=pltpu.HBM)
     dma = pltpu.SemaphoreType.DMA
     group = 9 // GROUPS * 128
-    big = (rhs, point_inverse, cam_block, precond, coupling)
+    big = (tile_index.T, tile_count.T, rhs, point_inverse, cam_block, precond, coupling)
     big = [pltpu.with_memory_space_constraint(x, pltpu.HBM) for x in big]
     return pl.pallas_call(
         functools.partial(kernel, n_cam, n_pts),
         out_shape=(jax.ShapeDtypeStruct(rhs.shape, F32), jax.ShapeDtypeStruct(rhs.shape, F32)),
-        in_specs=[whole, whole, hbm, hbm, hbm, hbm, hbm],
+        in_specs=[hbm] * 7,
         out_specs=(whole, whole),
         scratch_shapes=[
+            pltpu.VMEM((slots, tiles), jnp.int32),
+            pltpu.VMEM((1, tiles), jnp.int32),
             pltpu.VMEM(coupling.shape, BF16),
             pltpu.VMEM((9, 9, mine * 128), F32),
             pltpu.VMEM(precond.shape, F32),
@@ -573,6 +616,8 @@
             pltpu.VMEM((pairs, 144), F32),
             pltpu.VMEM((8 * half, 384), F32),
             pltpu.VMEM((pairs, 144), F32),
+            pltpu.VMEM((GROUPS, 8 * half, 144 // GROUPS), F32),
+            pltpu.VMEM((GROUPS, pairs, group), BF16),
             pltpu.VMEM((tiles // 2, 384), F32),
             pltpu.VMEM((tiles // 2, 384), F32),
             pltpu.VMEM((2, PIECES, n_cam, half, 384), BF16),
@@ -582,7 +627,7 @@
             pltpu.VMEM((2, GROUPS, n_pts // 2, mine, group), BF16),
             pltpu.VMEM((2, n_cam, 2, 128), F32),
             pltpu.VMEM((2, n_pts, 4, 128), F32),
-            dma((CHUNKS,)), dma, dma, dma, dma,
+            dma((CHUNKS,)), dma, dma, dma, dma, dma, dma,
             dma((PIECES, n_cam)), dma((2, PIECES, n_cam)),
             dma((2,)),
             dma((GROUPS,)), dma((GROUPS,)),
@@ -594,7 +639,7 @@
         compiler_params=pltpu.CompilerParams(
             collective_id=0, has_side_effects=True, vmem_limit_bytes=52 * 2**20
         ),
-    )(tile_index.T, tile_count.T, *big)
+    )(*big)
 
 
 def solution(mesh):

time: 79.2 us -> 76.9 us (0.971)
  local copies, waits for them, and re-layouts: 2.92 us -> 1.59 us
  Pallas kernels: 75.4 us -> 74.6 us
    unnamed x6 -> x2, local copies, waits for them, and re-layouts: 2.92 us -> 1.59 us
    pallas_call x1, Pallas kernels: 75.4 us -> 74.6 us  [per_device(): pl.pallas_call(functools.partial(kernel, n_cam, n_pts), out_shape=(jax.Sh...]
where the time goes in v5:
time: 76.9 us; the launch traced here: 76.8 us
  Pallas kernels  74.6 us (97%)
  local copies, waits for them, and re-layouts  1.59 us (2%)
    pallas_call x1, Pallas kernels, per_device(): pl.pallas_call(functools.partial(kernel, n_cam, n_pts), out_shape=(jax.Sh...  74.6 us
    unnamed x2, local copies, waits for them, and re-layouts  1.59 us

profile of v5, /device:TPU:1, one launch (start us, length us, event | category | flops | bytes accessed | tf_op | source)
XLA Modules:
  0.0 76.8 jit_solution(4750131810376697131)
XLA Ops:
  0.6 74.6 %shard_map.86 = (f32[9,8192]{1,0:T(8,128)S(1)}, f32[9,8192]{1,0:T(8,128)S(1)}) custom-call(s32[4,64]{1,0:T(4,128)} %bitcast.2, s32[1,64]{1,0:T(1,128)} %bitcast.3, f32[9,8192]{1,0:T(8,128)} %rhs_hbm.1, f32[3,3,4096]{2,1,0:T(4,128)} %inv_hbm.1, f32[9,9,8192]{2,1,0:T(8,128)} %cam_hbm.1, f32[9,9,8192]{2,1,0:T(8,128)} %pre_hbm.1, bf16[64,144,768]{2,1,0:T(8,128)(2,1)} %blk_hbm.1), custom_call_target="tpu_custom_call" | custom-call | tf_op jit(solution)/shard_map/pallas_call | solution.py:591
  75.2 0.8 %copy.11 = f32[9,8192]{1,0:T(8,128)} copy(f32[9,8192]{1,0:T(8,128)S(1)} %get-tuple-element.4) | data formatting | bytes 589824
  76.0 0.8 %copy.12 = f32[9,8192]{1,0:T(8,128)} copy(f32[9,8192]{1,0:T(8,128)S(1)} %get-tuple-element.5) | data formatting | bytes 589824

commit v6 on v5

--- a/solution.py
+++ b/solution.py
@@ -12,13 +12,16 @@
 BF16 = jnp.bfloat16
 CHUNKS = 16
 PIECES = 4
-UNROLL = 8
 GROUPS = 3
 MESH = pl.DeviceIdType.MESH
 
 
 def iota(shape, axis):
     return lax.broadcasted_iota(jnp.int32, shape, axis)
+
+
+def eight(j):
+    return slice(8 * j, 8 * j + 8) if isinstance(j, int) else pl.ds(pl.multiple_of(8 * j, 8), 8)
 
 
 def one_hot(where):
@@ -241,18 +244,20 @@
         parity = it % 2
         if it > 0:
             z_swap.wait()
-        for j in range(9):
-            wide = z_all[:, :, 128 * j : 128 * j + 128].astype(F32).reshape(blocks, 128)
-            picked = jnp.dot(pick[...], wide.astype(BF16), preferred_element_type=F32)
-            gath[:, 128 * j : 128 * j + 128] = (picked * mask[...]).astype(BF16)
-        rows[...] = jnp.dot(gath[...], fold[...], preferred_element_type=F32)
+        def gather(h):
+            some = slice(8 * per_piece * h, 8 * per_piece * (h + 1))
+            for j in range(9):
+                wide = z_all[:, :, 128 * j : 128 * j + 128].reshape(blocks, 128)
+                picked = jnp.dot(pick[some, :], wide, preferred_element_type=F32)
+                gath[some, 128 * j : 128 * j + 128] = (picked * mask[some, :]).astype(BF16)
+            rows[some, :] = jnp.dot(gath[some, :], fold[...], preferred_element_type=F32)
 
         def forward(j, h):
-            left = rows[pl.ds(pl.multiple_of(8 * j, 8), 8), :].astype(BF16)
+            left = rows[eight(j), :].astype(BF16)
             one = jnp.dot(left, blk[2 * j], preferred_element_type=F32)
             two = jnp.dot(left, blk[2 * j + 1], preferred_element_type=F32)
             both = jnp.where(diag, jnp.where(upper, one, two), 0.0)
-            mid[pl.ds(pl.multiple_of(8 * (j - h * per_piece), 8), 8), :] = (
+            mid[eight(j - h * per_piece), :] = (
                 both[:, :384] + both[:, 384:]
             )
 
@@ -265,6 +270,7 @@
             )
 
         for h in range(PIECES):
+            gather(h)
             if it == 0:
 
                 def forward_chunk(c, carry):
@@ -277,13 +283,8 @@
                 lax.fori_loop(h * some, (h + 1) * some, forward_chunk, 0)
             else:
 
-                def forward_some(c, carry):
-                    for k in range(UNROLL):
-                        forward(UNROLL * c + k, h)
-                    return carry
-
-                some = per_piece // UNROLL
-                lax.fori_loop(h * some, (h + 1) * some, forward_some, 0)
+                for k in range(per_piece):
+                    forward(h * per_piece + k, h)
             full = mid[...]
             high = full.astype(BF16)
             low = (full - high.astype(F32)).astype(BF16)
@@ -347,8 +348,8 @@
         def backward(j, lines, out, at):
             both = jnp.where(
                 upper[:, :384],
-                jnp.broadcast_to(even[pl.ds(j, 1), :], (8, 384)),
-                jnp.broadcast_to(odd[pl.ds(j, 1), :], (8, 384)),
+                jnp.broadcast_to(even[j : j + 1, :], (8, 384)),
+                jnp.broadcast_to(odd[j : j + 1, :], (8, 384)),
             )
             left = jnp.where(diag, jnp.concatenate([both, both], axis=1), 0.0).astype(BF16)
             contract = (((1,), (1,)), ((), ()))
@@ -411,14 +412,9 @@
 
             if h + 1 < PIECES:
 
-                def backward_some(c, carry):
-                    for k in range(UNROLL):
-                        j = UNROLL * c + k
-                        backward(j, slice(0, 144), contrib, pl.ds(pl.multiple_of(8 * j, 8), 8))
-                    return carry
-
-                some = per_piece // UNROLL
-                lax.fori_loop(h * some, (h + 1) * some, backward_some, 0)
+                for k in range(per_piece):
+                    j = h * per_piece + k
+                    backward(j, slice(0, 144), contrib, slice(8 * j, 8 * j + 8))
 
         def w_args(g):
             return (
@@ -574,6 +570,17 @@
             out_swap(1, res_out).wait()
 
 
+def hand_out(sol, res, sol_out, res_out, sem):
+    copies = [
+        pltpu.make_async_copy(sol, sol_out, sem.at[0]),
+        pltpu.make_async_copy(res, res_out, sem.at[1]),
+    ]
+    for copy in copies:
+        copy.start()
+    for copy in copies:
+        copy.wait()
+
+
 def per_device(n_cam, n_pts, rhs, cam_block, coupling, point_inverse, precond, tile_index, tile_count):
     tiles, slots = tile_index.shape
     cams = rhs.shape[1]
@@ -588,7 +595,7 @@
     group = 9 // GROUPS * 128
     big = (tile_index.T, tile_count.T, rhs, point_inverse, cam_block, precond, coupling)
     big = [pltpu.with_memory_space_constraint(x, pltpu.HBM) for x in big]
-    return pl.pallas_call(
+    results = pl.pallas_call(
         functools.partial(kernel, n_cam, n_pts),
         out_shape=(jax.ShapeDtypeStruct(rhs.shape, F32), jax.ShapeDtypeStruct(rhs.shape, F32)),
         in_specs=[hbm] * 7,
@@ -640,6 +647,14 @@
             collective_id=0, has_side_effects=True, vmem_limit_bytes=52 * 2**20
         ),
     )(*big)
+    return pl.pallas_call(
+        hand_out,
+        out_shape=(jax.ShapeDtypeStruct(rhs.shape, F32), jax.ShapeDtypeStruct(rhs.shape, F32)),
+        in_specs=[pl.BlockSpec(memory_space=pl.ANY)] * 2,
+        out_specs=(hbm, hbm),
+        scratch_shapes=[dma((2,))],
+        compiler_params=pltpu.CompilerParams(vmem_limit_bytes=2**20),
+    )(*results)
 
 
 def solution(mesh):

time: 76.9 us -> 77.3 us (level)
  Pallas kernels: 74.6 us -> 76.4 us
  local copies, waits for them, and re-layouts: 1.59 us -> 0 us
    unnamed x2 -> x0, local copies, waits for them, and re-layouts: 1.59 us -> none
    pallas_call x0 -> x1, Pallas kernels: none -> 0.99 us  [per_device(): pl.pallas_call(hand_out, out_shape=(jax.ShapeDtypeStruct(rhs.shape, F32),...]
    pallas_call x1, Pallas kernels: 74.6 us -> 75.4 us  [per_device(): pl.pallas_call(functools.partial(kernel, n_cam, n_pts), out_shape=(jax.Sh...]
where the time goes in v6:
time: 77.3 us; the launch traced here: 77.2 us
  Pallas kernels  76.4 us (99%)
  between operations  0.8 us (1%)
    pallas_call x1, Pallas kernels, per_device(): pl.pallas_call(functools.partial(kernel, n_cam, n_pts), out_shape=(jax.Sh...  75.4 us

profile of v6, /device:TPU:1, one launch (start us, length us, event | category | flops | bytes accessed | tf_op | source)
XLA Modules:
  0.0 77.2 jit_solution(1644281630046446721)
XLA Ops:
  0.6 75.4 %shard_map.86 = (f32[9,8192]{1,0:T(8,128)S(1)}, f32[9,8192]{1,0:T(8,128)S(1)}) custom-call(s32[4,64]{1,0:T(4,128)} %bitcast.2, s32[1,64]{1,0:T(1,128)} %bitcast.3, f32[9,8192]{1,0:T(8,128)} %rhs_hbm.1, f32[3,3,4096]{2,1,0:T(4,128)} %inv_hbm.1, f32[9,9,8192]{2,1,0:T(8,128)} %cam_hbm.1, f32[9,9,8192]{2,1,0:T(8,128)} %pre_hbm.1, bf16[64,144,768]{2,1,0:T(8,128)(2,1)} %blk_hbm.1), custom_call_target="tpu_custom_call" | custom-call | tf_op jit(solution)/shard_map/pallas_call | solution.py:598
  76.0 1.0 %shard_map.87 = (f32[9,8192]{1,0:T(8,128)}, f32[9,8192]{1,0:T(8,128)}) custom-call(f32[9,8192]{1,0:T(8,128)S(1)} %get-tuple-element.4.sol, f32[9,8192]{1,0:T(8,128)S(1)} %get-tuple-element.5.res), custom_call_target="tpu_custom_call" | custom-call | tf_op jit(solution)/shard_map/pallas_call | solution.py:650

commit v7 on v5

--- a/solution.py
+++ b/solution.py
@@ -107,12 +107,17 @@
             recv_sem=rsem.at[slot], device_id=(me_c, peer), device_id_type=MESH,
         )
 
+    side = 4
+    far = [(dy, dx) for dy in range(n_cam // side) for dx in range(side)][1:]
+    far.sort(key=lambda at: -min(at[0], n_cam // side - at[0]) - min(at[1], side - at[1]))
+    far = [
+        lax.rem(me_c // side + dy, n_cam // side) * side + lax.rem(lax.rem(me_c, side) + dx, side)
+        for dy, dx in far
+    ]
+
     def start_cam(*args):
-        def body(k, carry):
-            cam_copy_to(cam_peer(k), me_c, *args).start()
-            return carry
-
-        lax.fori_loop(1, n_cam, body, 0)
+        for peer in far:
+            cam_copy_to(peer, me_c, *args).start()
 
     def arrive_cam(*args):
         def body(k, carry):
@@ -433,7 +438,7 @@
             w_all[parity, g, me_z] = (
                 t_send[g, core].astype(F32) + t_recv[g].astype(F32)
             ).astype(BF16)
-            for k in range(1, n_z):
+            for k in (2, 1, 3):
                 along_z(k, me_z, *w_args(g)).start()
 
         t_swaps = []
@@ -574,6 +579,17 @@
             out_swap(1, res_out).wait()
 
 
+def hand_out(sol, res, sol_out, res_out, sem):
+    copies = [
+        pltpu.make_async_copy(sol, sol_out, sem.at[0]),
+        pltpu.make_async_copy(res, res_out, sem.at[1]),
+    ]
+    for copy in copies:
+        copy.start()
+    for copy in copies:
+        copy.wait()
+
+
 def per_device(n_cam, n_pts, rhs, cam_block, coupling, point_inverse, precond, tile_index, tile_count):
     tiles, slots = tile_index.shape
     cams = rhs.shape[1]
@@ -588,7 +604,7 @@
     group = 9 // GROUPS * 128
     big = (tile_index.T, tile_count.T, rhs, point_inverse, cam_block, precond, coupling)
     big = [pltpu.with_memory_space_constraint(x, pltpu.HBM) for x in big]
-    return pl.pallas_call(
+    results = pl.pallas_call(
         functools.partial(kernel, n_cam, n_pts),
         out_shape=(jax.ShapeDtypeStruct(rhs.shape, F32), jax.ShapeDtypeStruct(rhs.shape, F32)),
         in_specs=[hbm] * 7,
@@ -640,6 +656,14 @@
             collective_id=0, has_side_effects=True, vmem_limit_bytes=52 * 2**20
         ),
     )(*big)
+    return pl.pallas_call(
+        hand_out,
+        out_shape=(jax.ShapeDtypeStruct(rhs.shape, F32), jax.ShapeDtypeStruct(rhs.shape, F32)),
+        in_specs=[pl.BlockSpec(memory_space=pl.ANY)] * 2,
+        out_specs=(hbm, hbm),
+        scratch_shapes=[dma((2,))],
+        compiler_params=pltpu.CompilerParams(vmem_limit_bytes=2**20),
+    )(*results)
 
 
 def solution(mesh):

time: 76.9 us -> 75.5 us (0.982)
  local copies, waits for them, and re-layouts: 1.59 us -> 0 us
    unnamed x2 -> x0, local copies, waits for them, and re-layouts: 1.59 us -> none
    pallas_call x0 -> x1, Pallas kernels: none -> 0.99 us  [per_device(): pl.pallas_call(hand_out, out_shape=(jax.ShapeDtypeStruct(rhs.shape, F32),...]
    pallas_call x1, Pallas kernels: 74.6 us -> 73.6 us  [per_device(): pl.pallas_call(functools.partial(kernel, n_cam, n_pts), out_shape=(jax.Sh...]
where the time goes in v7:
time: 75.5 us; the launch traced here: 75.4 us
  Pallas kernels  74.6 us (99%)
  between operations  0.8 us (1%)
    pallas_call x1, Pallas kernels, per_device(): pl.pallas_call(functools.partial(kernel, n_cam, n_pts), out_shape=(jax.Sh...  73.6 us

profile of v7, /device:TPU:1, one launch (start us, length us, event | category | flops | bytes accessed | tf_op | source)
XLA Modules:
  0.0 75.4 jit_solution(467037191997818470)
XLA Ops:
  0.6 73.6 %shard_map.86 = (f32[9,8192]{1,0:T(8,128)S(1)}, f32[9,8192]{1,0:T(8,128)S(1)}) custom-call(s32[4,64]{1,0:T(4,128)} %bitcast.2, s32[1,64]{1,0:T(1,128)} %bitcast.3, f32[9,8192]{1,0:T(8,128)} %rhs_hbm.1, f32[3,3,4096]{2,1,0:T(4,128)} %inv_hbm.1, f32[9,9,8192]{2,1,0:T(8,128)} %cam_hbm.1, f32[9,9,8192]{2,1,0:T(8,128)} %pre_hbm.1, bf16[64,144,768]{2,1,0:T(8,128)(2,1)} %blk_hbm.1), custom_call_target="tpu_custom_call" | custom-call | tf_op jit(solution)/shard_map/pallas_call | solution.py:607
  74.3 1.0 %shard_map.87 = (f32[9,8192]{1,0:T(8,128)}, f32[9,8192]{1,0:T(8,128)}) custom-call(f32[9,8192]{1,0:T(8,128)S(1)} %get-tuple-element.4.sol, f32[9,8192]{1,0:T(8,128)S(1)} %get-tuple-element.5.res), custom_call_target="tpu_custom_call" | custom-call | tf_op jit(solution)/shard_map/pallas_call | solution.py:659

commit v8 on v7

--- a/solution.py
+++ b/solution.py
@@ -115,39 +115,29 @@
         for dy, dx in far
     ]
 
+    others = [pts_peer(k) for k in range(1, n_pts)]
+
     def start_cam(*args):
         for peer in far:
             cam_copy_to(peer, me_c, *args).start()
 
     def arrive_cam(*args):
-        def body(k, carry):
-            cam_copy_to(cam_peer(k), cam_peer(k), *args).wait_recv()
-            return carry
-
-        lax.fori_loop(1, n_cam, body, 0)
+        for peer in far[::-1]:
+            cam_copy_to(peer, peer, *args).wait_recv()
 
     def left_cam(*args):
-        def body(k, carry):
-            cam_copy_to(cam_peer(k), cam_peer(k), *args).wait_send()
-            return carry
-
-        lax.fori_loop(1, n_cam, body, 0)
+        for peer in far:
+            cam_copy_to(peer, peer, *args).wait_send()
 
     def start_pts(*args):
-        def body(k, carry):
-            pts_copy_to(pts_peer(k), me_p, *args).start()
-            return carry
-
-        lax.fori_loop(1, n_pts, body, 0)
+        for peer in others:
+            pts_copy_to(peer, me_p, *args).start()
 
     def wait_pts(*args):
-        def body(k, carry):
-            copy = pts_copy_to(pts_peer(k), pts_peer(k), *args)
+        for peer in others:
+            copy = pts_copy_to(peer, peer, *args)
             copy.wait_recv()
             copy.wait_send()
-            return carry
-
-        lax.fori_loop(1, n_pts, body, 0)
 
     def swap(src, dst, ssem, rsem):
         return pltpu.make_async_remote_copy(

time: 75.5 us -> 74.4 us (0.985)
  Pallas kernels: 74.6 us -> 73.5 us
    pallas_call x1, Pallas kernels: 73.6 us -> 72.5 us  [per_device(): pl.pallas_call(functools.partial(kernel, n_cam, n_pts), out_shape=(jax.Sh...]
where the time goes in v8:
time: 74.4 us; the launch traced here: 74.3 us
  Pallas kernels  73.5 us (99%)
  between operations  0.8 us (1%)
    pallas_call x1, Pallas kernels, per_device(): pl.pallas_call(functools.partial(kernel, n_cam, n_pts), out_shape=(jax.Sh...  72.5 us

profile of v8, /device:TPU:1, one launch (start us, length us, event | category | flops | bytes accessed | tf_op | source)
XLA Modules:
  0.0 74.3 jit_solution(5736725324661859276)
XLA Ops:
  0.6 72.5 %shard_map.86 = (f32[9,8192]{1,0:T(8,128)S(1)}, f32[9,8192]{1,0:T(8,128)S(1)}) custom-call(s32[4,64]{1,0:T(4,128)} %bitcast.2, s32[1,64]{1,0:T(1,128)} %bitcast.3, f32[9,8192]{1,0:T(8,128)} %rhs_hbm.1, f32[3,3,4096]{2,1,0:T(4,128)} %inv_hbm.1, f32[9,9,8192]{2,1,0:T(8,128)} %cam_hbm.1, f32[9,9,8192]{2,1,0:T(8,128)} %pre_hbm.1, bf16[64,144,768]{2,1,0:T(8,128)(2,1)} %blk_hbm.1), custom_call_target="tpu_custom_call" | custom-call | tf_op jit(solution)/shard_map/pallas_call | solution.py:597
  73.1 1.0 %shard_map.87 = (f32[9,8192]{1,0:T(8,128)}, f32[9,8192]{1,0:T(8,128)}) custom-call(f32[9,8192]{1,0:T(8,128)S(1)} %get-tuple-element.4.sol, f32[9,8192]{1,0:T(8,128)S(1)} %get-tuple-element.5.res), custom_call_target="tpu_custom_call" | custom-call | tf_op jit(solution)/shard_map/pallas_call | solution.py:649

commit v9 on v8

--- a/solution.py
+++ b/solution.py
@@ -63,49 +63,8 @@
 
     barrier = pltpu.get_barrier_semaphore()
 
-    def cam_peer(k):
-        return lax.rem(me_c + k, n_cam)
-
     def pts_peer(k):
         return lax.rem(me_p + k, n_pts)
-
-    def greet_cam(k, carry):
-        pl.semaphore_signal(barrier, inc=1, device_id=(cam_peer(k), me_p), device_id_type=MESH)
-        return carry
-
-    def greet_pts(k, carry):
-        pl.semaphore_signal(barrier, inc=1, device_id=(me_c, pts_peer(k)), device_id_type=MESH)
-        return carry
-
-    lax.fori_loop(1, n_cam, greet_cam, 0)
-    lax.fori_loop(1, n_pts, greet_pts, 0)
-
-    idx_copy = pltpu.make_async_copy(idx_hbm, idx_ref, idx_sem)
-    count_copy = pltpu.make_async_copy(count_hbm, count_ref, count_sem)
-    idx_copy.start()
-    count_copy.start()
-    rhs_copy.start()
-    pre_copy.start()
-
-    def start_chunk(c, carry):
-        blk_copy(c).start()
-        return carry
-
-    lax.fori_loop(0, CHUNKS, start_chunk, 0)
-    inv_copy.start()
-    cam_copy.start()
-
-    def cam_copy_to(peer, slot, src, dst, ssem, rsem):
-        return pltpu.make_async_remote_copy(
-            src_ref=src(peer), dst_ref=dst(slot), send_sem=ssem.at[peer],
-            recv_sem=rsem.at[slot], device_id=(peer, me_p), device_id_type=MESH,
-        )
-
-    def pts_copy_to(peer, slot, src, dst, ssem, rsem):
-        return pltpu.make_async_remote_copy(
-            src_ref=src(peer), dst_ref=dst(slot), send_sem=ssem.at[peer],
-            recv_sem=rsem.at[slot], device_id=(me_c, peer), device_id_type=MESH,
-        )
 
     side = 4
     far = [(dy, dx) for dy in range(n_cam // side) for dx in range(side)][1:]
@@ -116,6 +75,38 @@
     ]
 
     others = [pts_peer(k) for k in range(1, n_pts)]
+
+    for peer in far:
+        pl.semaphore_signal(barrier, inc=1, device_id=(peer, me_p), device_id_type=MESH)
+    for peer in others:
+        pl.semaphore_signal(barrier, inc=1, device_id=(me_c, peer), device_id_type=MESH)
+
+    idx_copy = pltpu.make_async_copy(idx_hbm, idx_ref, idx_sem)
+    count_copy = pltpu.make_async_copy(count_hbm, count_ref, count_sem)
+    idx_copy.start()
+    count_copy.start()
+    rhs_copy.start()
+    pre_copy.start()
+
+    def start_chunk(c, carry):
+        blk_copy(c).start()
+        return carry
+
+    lax.fori_loop(0, CHUNKS, start_chunk, 0)
+    inv_copy.start()
+    cam_copy.start()
+
+    def cam_copy_to(peer, slot, src, dst, ssem, rsem):
+        return pltpu.make_async_remote_copy(
+            src_ref=src(peer), dst_ref=dst(slot), send_sem=ssem.at[peer],
+            recv_sem=rsem.at[slot], device_id=(peer, me_p), device_id_type=MESH,
+        )
+
+    def pts_copy_to(peer, slot, src, dst, ssem, rsem):
+        return pltpu.make_async_remote_copy(
+            src_ref=src(peer), dst_ref=dst(slot), send_sem=ssem.at[peer],
+            recv_sem=rsem.at[slot], device_id=(me_c, peer), device_id_type=MESH,
+        )
 
     def start_cam(*args):
         for peer in far:

time: 74.4 us -> 74.4 us (level)
  no operation moved by 1% of the time
where the time goes in v9:
time: 74.4 us; the launch traced here: 74.2 us
  Pallas kernels  73.4 us (99%)
  between operations  0.8 us (1%)
    pallas_call x1, Pallas kernels, per_device(): pl.pallas_call(functools.partial(kernel, n_cam, n_pts), out_shape=(jax.Sh...  72.5 us

profile of v9, /device:TPU:1, one launch (start us, length us, event | category | flops | bytes accessed | tf_op | source)
XLA Modules:
  0.0 74.2 jit_solution(4421515036859994443)
XLA Ops:
  0.6 72.5 %shard_map.86 = (f32[9,8192]{1,0:T(8,128)S(1)}, f32[9,8192]{1,0:T(8,128)S(1)}) custom-call(s32[4,64]{1,0:T(4,128)} %bitcast.2, s32[1,64]{1,0:T(1,128)} %bitcast.3, f32[9,8192]{1,0:T(8,128)} %rhs_hbm.1, f32[3,3,4096]{2,1,0:T(4,128)} %inv_hbm.1, f32[9,9,8192]{2,1,0:T(8,128)} %cam_hbm.1, f32[9,9,8192]{2,1,0:T(8,128)} %pre_hbm.1, bf16[64,144,768]{2,1,0:T(8,128)(2,1)} %blk_hbm.1), custom_call_target="tpu_custom_call" | custom-call | tf_op jit(solution)/shard_map/pallas_call | solution.py:588
  73.1 1.0 %shard_map.87 = (f32[9,8192]{1,0:T(8,128)}, f32[9,8192]{1,0:T(8,128)}) custom-call(f32[9,8192]{1,0:T(8,128)S(1)} %get-tuple-element.4.sol, f32[9,8192]{1,0:T(8,128)S(1)} %get-tuple-element.5.res), custom_call_target="tpu_custom_call" | custom-call | tf_op jit(solution)/shard_map/pallas_call | solution.py:640
